TPU v7x, 128 devices: a whole 4x4x4 slice. The times are simulated.
128 devices in a mesh: by: 8 (over z, core), bx: 16 (over x, y).
Axes of the slice: x: 4, y: 4, z: 4, core: 2. Of those that a mesh axis runs over, the one named last changes fastest.
Arguments:
- tracers: float32 [20, 512, 16, 2048], P(None, ('by', 'bx')), may hold values from 0 to 1
- vertical_speed: float32 [20, 512, 2048], P(None, ('by', 'bx')), may hold values from -0.4 to 0.4
- diffusivity: float32 [20, 512, 2048], P(None, ('by', 'bx')), may hold values from 0.02 to 2
- buoyancy_force: bfloat16 [20, 512, 2048], P(None, ('by', 'bx')), may hold values from -2.1 to 2.1
- wet_levels: int32 [512, 2048], P(('by', 'bx')), may hold values from 0 to 20
- surface_patch: int32 [512, 2048], P(('by', 'bx')), may hold values from 0 to 15
- prior_height: float32 [512, 2048], P(('by', 'bx')), may hold values from -5 to 5
- land_mask: int32 [512, 16, 128], P(('by', 'bx')), may hold values 0 or 1
- baroclinic_map: int32 [512], replicated, may hold values from 0 to 511, as said below
- barotropic_map: int32 [512], replicated, may hold values from 0 to 511, as said below
Outputs:
- new_tracers: float32 [20, 512, 16, 2048], P(None, ('by', 'bx'))
- surface_height: float32 [512, 16, 128], P(('by', 'bx'))
Inputs may be any that keep to these rules, and one draw needn't show every extreme that they name: baroclinic_map[s] is the geographic block held in baroclinic slot s, blocks numbered row by row with 64 to a block row; it lies in block row s // 64, and every block appears once. barotropic_map[s] is the geographic block held in barotropic slot s, blocks numbered row by row with 64 to a block row; it lies in block row s // 64, and every block appears once.
All inputs are finite; a program needn't handle non-finite values. No bound on the sum of `land_mask` on one device may be relied on, other than what follows from the above.
Results may differ from a plain program's by a relative error of at most 0.0003.
Values sent between devices are 32-bit elements; how exact they have to be, the bound alone decides.
A program may use at most 128 MiB of HBM per device.

v0:
```python
import jax
import jax.numpy as jnp
from jax import lax
from jax.sharding import PartitionSpec as P

ITERS = 6


RESTORE = 0.5
SURFACE = 0.1
FACE_SCALE = 2.0
PRECISE = lax.Precision.HIGHEST


def padded_2(block, sides, width):
    for axis, dim in sides:
        count = lax.axis_size(axis)
        forward = [(i, i + 1) for i in range(count - 1)]
        backward = [(target, source) for source, target in forward]
        low = lax.ppermute(
            lax.slice_in_dim(block, block.shape[dim] - width, None, axis=dim), axis, forward
        )
        high = lax.ppermute(lax.slice_in_dim(block, 0, width, axis=dim), axis, backward)
        block = jnp.concatenate([low, block, high], axis=dim)
    return block


def column_step(tracers, vertical_speed, diffusivity, wet_levels, surface_patch):
    depth_index = lax.broadcasted_iota(jnp.int32, vertical_speed.shape, 0)
    wet_level = (depth_index < wet_levels[None]).astype(jnp.float32)
    open_faces = (depth_index + 1 < wet_levels[None]).astype(jnp.float32)
    speed_open = (vertical_speed * open_faces)[:, :, None]
    shifted_up = jnp.concatenate([tracers[1:], jnp.zeros_like(tracers[:1])], axis=0)
    flux_below = jnp.maximum(speed_open, 0.0) * shifted_up + jnp.minimum(speed_open, 0.0) * tracers
    flux_above = jnp.concatenate([jnp.zeros_like(flux_below[:1]), flux_below[:-1]], axis=0)
    advected = wet_level[:, :, None] * (tracers + flux_below - flux_above)
    mixing = diffusivity * open_faces
    mixing_above = jnp.concatenate([jnp.zeros_like(mixing[:1]), mixing[:-1]], axis=0)
    surface_row = (depth_index == 0).astype(jnp.float32) * wet_level * RESTORE
    diagonal = 1.0 + mixing + mixing_above + surface_row
    tracer_ids = lax.broadcasted_iota(jnp.int32, (1, tracers.shape[2], 1), 1)
    targets = (surface_patch[:, None, :] == tracer_ids).astype(jnp.float32)
    right_side = advected + surface_row[:, :, None] * targets[None]

    def forward(carry, layer):
        ratio_prev, value_prev = carry
        lower_band, diag_now, upper_band, right_now = layer
        pivot_now = diag_now - lower_band * ratio_prev
        ratio_now = upper_band / pivot_now
        value_now = (right_now - lower_band[:, None] * value_prev) / pivot_now[:, None]
        return ((ratio_now, value_now), (ratio_now, value_now))

    start_carry = (
        jnp.zeros(mixing.shape[1:], jnp.float32),
        jnp.zeros(tracers.shape[1:], jnp.float32),
    )
    ignored, (ratios, values) = lax.scan(
        forward, start_carry, (-mixing_above, diagonal, -mixing, right_side)
    )

    def backward(following, layer):
        ratio_now, value_now = layer
        solved_now = value_now - ratio_now[:, None] * following
        return (solved_now, solved_now)

    ignored_too, solved = lax.scan(
        backward, jnp.zeros(tracers.shape[1:], jnp.float32), (ratios, values), reverse=True
    )
    return solved


def local(
    tracers,
    vertical_speed,
    diffusivity,
    buoyancy_force,
    wet_levels,
    surface_patch,
    prior_height,
    land_mask,
    baroclinic_map,
    barotropic_map,
):
    blocks = wet_levels.shape[0]
    block_rows = land_mask.shape[1]
    block_cols = land_mask.shape[2]
    levels = vertical_speed.shape[0]
    band_row = lax.axis_index("by")
    column = lax.axis_index("bx")
    band_width = blocks * lax.axis_size("bx")
    band_first_slot = band_row * band_width
    clinic_band = (
        lax.dynamic_slice_in_dim(baroclinic_map, band_first_slot, band_width) - band_first_slot
    )
    tropic_band = (
        lax.dynamic_slice_in_dim(barotropic_map, band_first_slot, band_width) - band_first_slot
    )
    my_columns = lax.dynamic_slice_in_dim(tropic_band, column * blocks, blocks)
    depth_index = lax.broadcasted_iota(jnp.int32, buoyancy_force.shape, 0)
    wet_level = (depth_index < wet_levels[None]).astype(jnp.float32)
    forcing = jnp.sum(wet_level * buoyancy_force.astype(jnp.float32), axis=0)
    payload = jnp.stack([forcing, wet_levels.astype(jnp.float32), prior_height], axis=0)
    selector = (clinic_band[None, :] == my_columns[:, None]).astype(jnp.float32)
    relaid = jnp.einsum(
        "jt,qtc->qjc",
        selector,
        lax.all_gather(payload, "bx", axis=1, tiled=True),
        precision=PRECISE,
    )
    new_tracers = column_step(tracers, vertical_speed, diffusivity, wet_levels, surface_patch)
    shape_flat = (blocks, block_rows, block_cols)
    ocean_mask = land_mask.astype(jnp.float32)
    depth_field = relaid[1].reshape(shape_flat)
    source = ocean_mask * relaid[0].reshape(shape_flat)
    first_guess = ocean_mask * relaid[2].reshape(shape_flat)
    west_pick = (tropic_band[None, :] == (my_columns[:, None] - 1) % band_width).astype(jnp.float32)
    east_pick = (tropic_band[None, :] == (my_columns[:, None] + 1) % band_width).astype(jnp.float32)
    band_slots = lax.broadcasted_iota(jnp.int32, (band_width, 1), 0)
    geo_pick = (tropic_band[None, :] == band_slots).astype(jnp.float32)
    my_pick = (band_slots[:, 0][None, :] == my_columns[:, None]).astype(jnp.float32)

    def extend(field_blocks):
        edge_cols = jnp.stack([field_blocks[..., 0], field_blocks[..., -1]], axis=2)
        edge_rows = jnp.stack([field_blocks[..., 0, :], field_blocks[..., -1, :]], axis=2)
        gathered_cols, gathered_rows = (
            lax.all_gather(edge_cols, "bx", axis=1, tiled=True),
            lax.all_gather(edge_rows, "bx", axis=1, tiled=True),
        )
        geo_rows = jnp.einsum("ct,qtsw->sqcw", geo_pick, gathered_rows, precision=PRECISE)
        beside = padded_2(geo_rows, (("by", 0),), 1)
        north_side = jnp.einsum("jc,qcw->qjw", my_pick, beside[0], precision=PRECISE)
        south_side = jnp.einsum("jc,qcw->qjw", my_pick, beside[3], precision=PRECISE)
        west_side = jnp.einsum("jt,qth->qjh", west_pick, gathered_cols[:, :, 1], precision=PRECISE)
        east_side = jnp.einsum("jt,qth->qjh", east_pick, gathered_cols[:, :, 0], precision=PRECISE)
        middle = jnp.concatenate([west_side[..., None], field_blocks, east_side[..., None]], axis=3)
        north_row = jnp.pad(north_side, ((0, 0), (0, 0), (1, 1)))[:, :, None, :]
        south_row = jnp.pad(south_side, ((0, 0), (0, 0), (1, 1)))[:, :, None, :]
        return jnp.concatenate([north_row, middle, south_row], axis=2)

    statics = extend(jnp.stack([depth_field, ocean_mask], axis=0))
    depth_padded = statics[0]
    ocean_padded = statics[1]
    face_factor = FACE_SCALE / levels

    def face_weight(depth_other, ocean_other):
        return face_factor * jnp.minimum(depth_field, depth_other) * ocean_mask * ocean_other

    east_face = face_weight(depth_padded[:, 1:-1, 2:], ocean_padded[:, 1:-1, 2:])
    west_face = face_weight(depth_padded[:, 1:-1, :-2], ocean_padded[:, 1:-1, :-2])
    south_face = face_weight(depth_padded[:, 2:, 1:-1], ocean_padded[:, 2:, 1:-1])
    north_face = face_weight(depth_padded[:, :-2, 1:-1], ocean_padded[:, :-2, 1:-1])
    centre_weight = SURFACE * ocean_mask + (1.0 - ocean_mask)
    precond_diagonal = centre_weight + east_face + west_face + south_face + north_face

    def operate(field_blocks):
        padded = extend(field_blocks[None])[0]
        centre = centre_weight * field_blocks
        result = centre + east_face * (field_blocks - padded[:, 1:-1, 2:])
        result = result + west_face * (field_blocks - padded[:, 1:-1, :-2])
        result = result + south_face * (field_blocks - padded[:, 2:, 1:-1])
        return result + north_face * (field_blocks - padded[:, :-2, 1:-1])

    solution = first_guess
    residual = source - operate(solution)
    precond = residual / precond_diagonal

    def weighted(residual_now, precond_now):
        return lax.psum(jnp.sum(residual_now * precond_now), ("by", "bx"))

    direction = precond
    norm_now = weighted(residual, precond)
    for step_index in range(ITERS):
        image_field = operate(direction)
        step_size = norm_now / lax.psum(jnp.sum(direction * image_field), ("by", "bx"))
        solution = solution + step_size * direction
        residual = residual - step_size * image_field
        if step_index + 1 < ITERS:
            precond = residual / precond_diagonal
            norm_next = weighted(residual, precond)
            direction = precond + norm_next / norm_now * direction
            norm_now = norm_next
    return (new_tracers, solution)


def solution(mesh):
    return jax.shard_map(
        local,
        mesh=mesh,
        in_specs=(
            P(None, ("by", "bx"), None, None),
            P(None, ("by", "bx"), None),
            P(None, ("by", "bx"), None),
            P(None, ("by", "bx"), None),
            P(("by", "bx"), None),
            P(("by", "bx"), None),
            P(("by", "bx"), None),
            P(("by", "bx"), None, None),
            P(),
            P(),
        ),
        out_specs=(P(None, ("by", "bx"), None, None), P(("by", "bx"), None, None)),
        check_vma=False,
    )
```

profile of v0, /device:TPU:1, one launch (start us, length us, event | category | flops | bytes accessed | tf_op | source)
XLA Modules:
  0.0 1332.6 jit_solution(10514332008034676761)
XLA Ops:
  8.0 2.8 fusion.5
  10.9 2.7 pad_negate_fusion
  16.1 3.8 slice-done
  19.9 9.8 multiply_add_fusion.1
  29.7 9.2 slice.433
  38.9 15.5 %multiply_add_fusion = f32[20,4,16,2048]{3,2,1,0:T(8,128)} fusion(f32[19,4,16,2048]{3,2,1,0:T(8,128)} %slice.433, f32[20,4,16,2048]{3,2,1,0:T(8,128)} %param.14, f32[20,4,16,2048]{3,2,1,0:T(8,128)} %multiply_add_fusion.1, f32[4,16,2048]{2,1,0:T(8,128)S(1)} %fusion.3, f32[20,4,2048]{2,1,0:T(4,128)S(1)} %get-tuple-element.335, f32[20,4,2048]{2,1,0:T(4,128)S(1)} %fusion.2), kind=kLoop, calls=%fused_computation.13 | loop fusion | flops 13107200 | bytes 43253760 | tf_op jit(solution)/shard_map/add | solution.py:43
  54.4 5.3 broadcast.122.clone
  59.9 58.2 %while.34 = (s32[]{:T(128)}, f32[4,2048]{1,0:T(4,128)S(1)}, f32[4,16,2048]{2,1,0:T(8,128)S(1)}, f32[20,4,2048]{2,1,0:T(4,128)S(1)}, f32[20,4,16,2048]{3,2,1,0:T(...) while((s32[]{:T(128)}, f32[4,2048]{1,0:T(4,128)S(1)}, ...), condition=%wide.region_1.2_spmd.clone, body=%wide.region_0.0_spmd.clone.sunk | while | flops 557059 | bytes 2425468 | solution.py:57
  119.7 3.0 convolution_bitcast_fusion
  123.1 19.4 %all_gather.55 = f32[1,64,2,16]{3,2,0,1:T(2,128)S(1)} all-gather(f32[1,4,2,16]{3,2,0,1:T(2,128)S(1)} %copy.201), channel_id=1, replica_groups=mesh['by'=8,'bx'=16] {'bx'}, dimensions={1}, use_global_device_ids=true | all-gather | bytes 8704 | tf_op jit(solution)/shard_map/all_gather | solution.py:126
  142.9 17.5 %all_gather.54 = f32[1,64,2,128]{3,2,0,1:T(2,128)S(1)} all-gather(f32[1,4,2,128]{3,2,0,1:T(2,128)S(1)} %maximum_bitcast_fusion.7), channel_id=1, replica_groups=mesh['by'=8,'bx'=16] {'bx'}, dimensions={1}, use_global_device_ids=true | all-gather | bytes 69632 | tf_op jit(solution)/shard_map/all_gather | solution.py:127
  160.6 14.6 %collective-permute-start.2 = (f32[1,1,64,128]{3,2,0,1:T(8,128)S(1)}, f32[1,1,64,128]{3,2,0,1:T(8,128)S(1)}, u32[]{:S(2)}, u32[]{:S(2)}) collective-permute-start(f32[1,1,64,128]{3,2,0,1:T(8,128)S(1)} %get-tuple-element.331), channel_id=1, source_target_pairs={{0,16},{16,32},{32,48},{48,64},{64,80},{80,96},{96,112},{1,17},{17... | collective-permute-start | bytes 98312 | tf_op jit(solution)/shard_map/ppermute | solution.py:20
  177.4 16.0 %all_gather.53 = f32[2,64,2,16]{3,2,0,1:T(2,128)S(1)} all-gather(f32[2,4,2,16]{3,2,0,1:T(2,128)S(1)} %copy.191), channel_id=1, replica_groups=mesh['by'=8,'bx'=16] {'bx'}, dimensions={1}, use_global_device_ids=true | all-gather | bytes 17408 | tf_op jit(solution)/shard_map/all_gather | solution.py:126
  193.9 17.6 %all_gather.52 = f32[2,64,2,128]{3,2,0,1:T(2,128)S(1)} all-gather(f32[2,4,2,128]{3,2,0,1:T(2,128)S(1)} %fusion.130), channel_id=1, replica_groups=mesh['by'=8,'bx'=16] {'bx'}, dimensions={1}, use_global_device_ids=true | all-gather | bytes 139264 | tf_op jit(solution)/shard_map/all_gather | solution.py:127
  212.5 14.6 %collective-permute-start = (f32[1,2,64,128]{3,2,0,1:T(8,128)S(1)}, f32[1,2,64,128]{3,2,0,1:T(8,128)S(1)}, u32[]{:S(2)}, u32[]{:S(2)}) collective-permute-start(f32[1,2,64,128]{3,2,0,1:T(8,128)S(1)} %get-tuple-element.298), channel_id=1, source_target_pairs={{0,16},{16,32},{32,48},{48,64},{64,80},{80,96},{96,112},{1,17},{17... | collective-permute-start | bytes 196616 | tf_op jit(solution)/shard_map/ppermute | solution.py:20
  230.0 2.7 collective-permute-done.1
  233.5 16.3 %all_gather.57 = f32[1,64,2,16]{3,2,0,1:T(2,128)S(1)} all-gather(f32[1,4,2,16]{3,2,0,1:T(2,128)S(1)} %copy.208), channel_id=1, replica_groups=mesh['by'=8,'bx'=16] {'bx'}, dimensions={1}, use_global_device_ids=true | all-gather | bytes 8704 | tf_op jit(solution)/shard_map/all_gather | solution.py:126
  250.1 17.4 %all_gather.56 = f32[1,64,2,128]{3,2,0,1:T(2,128)S(1)} all-gather(f32[1,4,2,128]{3,2,0,1:T(2,128)S(1)} %maximum_bitcast_fusion.8), channel_id=1, replica_groups=mesh['by'=8,'bx'=16] {'bx'}, dimensions={1}, use_global_device_ids=true | all-gather | bytes 69632 | tf_op jit(solution)/shard_map/all_gather | solution.py:127
  267.7 12.9 collective-permute-start.4
  283.2 3.0 collective-permute-done.5
  287.4 63.4 %all-reduce.19 = (f32[]{:T(128)}, f32[]{:T(128)}) all-reduce(f32[]{:T(128)} %get-tuple-element.217, f32[]{:T(128)} %get-tuple-element.216), channel_id=1, replica_groups=mesh['by'=8,'bx'=16] {'by','bx'}, use_global_device_ids=true, to_apply=%region_6.7 | all-reduce | flops 2 | bytes 16 | tf_op jit(solution)/shard_map/psum | solution.py:168
  352.7 63.8 %psum.86 = f32[]{:T(128)} all-reduce(f32[]{:T(128)} %get-tuple-element.276), channel_id=1, replica_groups=mesh['by'=8,'bx'=16] {'by','bx'}, use_global_device_ids=true, to_apply=%region_10.11 | all-reduce | flops 1 | bytes 8 | tf_op jit(solution)/shard_map/psum | solution.py:168
  418.1 16.0 %all_gather.59 = f32[1,64,2,16]{3,2,0,1:T(2,128)S(1)} all-gather(f32[1,4,2,16]{3,2,0,1:T(2,128)S(1)} %copy.215), channel_id=1, replica_groups=mesh['by'=8,'bx'=16] {'bx'}, dimensions={1}, use_global_device_ids=true | all-gather | bytes 8704 | tf_op jit(solution)/shard_map/all_gather | solution.py:126
  434.3 17.6 %all_gather.58 = f32[1,64,2,128]{3,2,0,1:T(2,128)S(1)} all-gather(f32[1,4,2,128]{3,2,0,1:T(2,128)S(1)} %maximum_bitcast_fusion.9), channel_id=1, replica_groups=mesh['by'=8,'bx'=16] {'bx'}, dimensions={1}, use_global_device_ids=true | all-gather | bytes 69632 | tf_op jit(solution)/shard_map/all_gather | solution.py:127
  452.1 13.6 %collective-permute-start.6 = (f32[1,1,64,128]{3,2,0,1:T(8,128)S(1)}, f32[1,1,64,128]{3,2,0,1:T(8,128)S(1)}, u32[]{:S(2)}, u32[]{:S(2)}) collective-permute-start(f32[1,1,64,128]{3,2,0,1:T(8,128)S(1)} %get-tuple-element.321), channel_id=1, source_target_pairs={{0,16},{16,32},{32,48},{48,64},{64,80},{80,96},{96,112},{1,17},{17... | collective-permute-start | bytes 98312 | tf_op jit(solution)/shard_map/ppermute | solution.py:20
  468.2 3.0 collective-permute-done.7
  472.4 63.4 %psum.87 = f32[]{:T(128)} all-reduce(f32[]{:T(128)} %get-tuple-element.274), channel_id=1, replica_groups=mesh['by'=8,'bx'=16] {'by','bx'}, use_global_device_ids=true, to_apply=%region_12.13 | all-reduce | flops 1 | bytes 8 | tf_op jit(solution)/shard_map/psum | solution.py:174
  537.7 62.6 %psum.88 = f32[]{:T(128)} all-reduce(f32[]{:T(128)} %get-tuple-element.271), channel_id=1, replica_groups=mesh['by'=8,'bx'=16] {'by','bx'}, use_global_device_ids=true, to_apply=%region_14.15 | all-reduce | flops 1 | bytes 8 | tf_op jit(solution)/shard_map/psum | solution.py:168
  601.9 17.5 %all_gather.61 = f32[1,64,2,16]{3,2,0,1:T(2,128)S(1)} all-gather(f32[1,4,2,16]{3,2,0,1:T(2,128)S(1)} %copy.222), channel_id=1, replica_groups=mesh['by'=8,'bx'=16] {'bx'}, dimensions={1}, use_global_device_ids=true | all-gather | bytes 8704 | tf_op jit(solution)/shard_map/all_gather | solution.py:126
  619.7 16.0 %all_gather.60 = f32[1,64,2,128]{3,2,0,1:T(2,128)S(1)} all-gather(f32[1,4,2,128]{3,2,0,1:T(2,128)S(1)} %maximum_bitcast_fusion.10), channel_id=1, replica_groups=mesh['by'=8,'bx'=16] {'bx'}, dimensions={1}, use_global_device_ids=true | all-gather | bytes 69632 | tf_op jit(solution)/shard_map/all_gather | solution.py:127
  635.9 15.2 %collective-permute-start.8 = (f32[1,1,64,128]{3,2,0,1:T(8,128)S(1)}, f32[1,1,64,128]{3,2,0,1:T(8,128)S(1)}, u32[]{:S(2)}, u32[]{:S(2)}) collective-permute-start(f32[1,1,64,128]{3,2,0,1:T(8,128)S(1)} %get-tuple-element.317), channel_id=1, source_target_pairs={{0,16},{16,32},{32,48},{48,64},{64,80},{80,96},{96,112},{1,17},{17... | collective-permute-start | bytes 98312 | tf_op jit(solution)/shard_map/ppermute | solution.py:20
  653.7 3.0 collective-permute-done.9
  657.8 62.1 %psum.89 = f32[]{:T(128)} all-reduce(f32[]{:T(128)} %get-tuple-element.269), channel_id=1, replica_groups=mesh['by'=8,'bx'=16] {'by','bx'}, use_global_device_ids=true, to_apply=%region_16.17 | all-reduce | flops 1 | bytes 8 | tf_op jit(solution)/shard_map/psum | solution.py:174
  721.9 64.2 %psum.90 = f32[]{:T(128)} all-reduce(f32[]{:T(128)} %get-tuple-element.266), channel_id=1, replica_groups=mesh['by'=8,'bx'=16] {'by','bx'}, use_global_device_ids=true, to_apply=%region_18.19 | all-reduce | flops 1 | bytes 8 | tf_op jit(solution)/shard_map/psum | solution.py:168
  787.6 16.1 %all_gather.63 = f32[1,64,2,16]{3,2,0,1:T(2,128)S(1)} all-gather(f32[1,4,2,16]{3,2,0,1:T(2,128)S(1)} %copy.229), channel_id=1, replica_groups=mesh['by'=8,'bx'=16] {'bx'}, dimensions={1}, use_global_device_ids=true | all-gather | bytes 8704 | tf_op jit(solution)/shard_map/all_gather | solution.py:126
  804.0 17.5 %all_gather.62 = f32[1,64,2,128]{3,2,0,1:T(2,128)S(1)} all-gather(f32[1,4,2,128]{3,2,0,1:T(2,128)S(1)} %maximum_bitcast_fusion.11), channel_id=1, replica_groups=mesh['by'=8,'bx'=16] {'bx'}, dimensions={1}, use_global_device_ids=true | all-gather | bytes 69632 | tf_op jit(solution)/shard_map/all_gather | solution.py:127
  821.6 12.6 collective-permute-start.10
  834.7 2.7 collective-permute-start.11
  837.6 2.3 collective-permute-done.11
  841.0 64.5 %psum.91 = f32[]{:T(128)} all-reduce(f32[]{:T(128)} %get-tuple-element.264), channel_id=1, replica_groups=mesh['by'=8,'bx'=16] {'by','bx'}, use_global_device_ids=true, to_apply=%region_20.21 | all-reduce | flops 1 | bytes 8 | tf_op jit(solution)/shard_map/psum | solution.py:174
  907.5 62.5 %psum.92 = f32[]{:T(128)} all-reduce(f32[]{:T(128)} %get-tuple-element.261), channel_id=1, replica_groups=mesh['by'=8,'bx'=16] {'by','bx'}, use_global_device_ids=true, to_apply=%region_22.23 | all-reduce | flops 1 | bytes 8 | tf_op jit(solution)/shard_map/psum | solution.py:168
  971.5 17.6 %all_gather.65 = f32[1,64,2,16]{3,2,0,1:T(2,128)S(1)} all-gather(f32[1,4,2,16]{3,2,0,1:T(2,128)S(1)} %copy.236), channel_id=1, replica_groups=mesh['by'=8,'bx'=16] {'bx'}, dimensions={1}, use_global_device_ids=true | all-gather | bytes 8704 | tf_op jit(solution)/shard_map/all_gather | solution.py:126
  989.4 16.0 %all_gather.64 = f32[1,64,2,128]{3,2,0,1:T(2,128)S(1)} all-gather(f32[1,4,2,128]{3,2,0,1:T(2,128)S(1)} %maximum_bitcast_fusion.12), channel_id=1, replica_groups=mesh['by'=8,'bx'=16] {'bx'}, dimensions={1}, use_global_device_ids=true | all-gather | bytes 69632 | tf_op jit(solution)/shard_map/all_gather | solution.py:127
  1005.6 15.0 %collective-permute-start.12 = (f32[1,1,64,128]{3,2,0,1:T(8,128)S(1)}, f32[1,1,64,128]{3,2,0,1:T(8,128)S(1)}, u32[]{:S(2)}, u32[]{:S(2)}) collective-permute-start(f32[1,1,64,128]{3,2,0,1:T(8,128)S(1)} %get-tuple-element.309), channel_id=1, source_target_pairs={{0,16},{16,32},{32,48},{48,64},{64,80},{80,96},{96,112},{1,17},{17... | collective-permute-start | bytes 98312 | tf_op jit(solution)/shard_map/ppermute | solution.py:20
  1023.2 3.0 collective-permute-done.13
  1027.3 62.1 %psum.93 = f32[]{:T(128)} all-reduce(f32[]{:T(128)} %get-tuple-element.259), channel_id=1, replica_groups=mesh['by'=8,'bx'=16] {'by','bx'}, use_global_device_ids=true, to_apply=%region_24.25 | all-reduce | flops 1 | bytes 8 | tf_op jit(solution)/shard_map/psum | solution.py:174
  1091.5 64.2 %psum.94 = f32[]{:T(128)} all-reduce(f32[]{:T(128)} %multiply_reduce_fusion), channel_id=1, replica_groups=mesh['by'=8,'bx'=16] {'by','bx'}, use_global_device_ids=true, to_apply=%region_26.27 | all-reduce | flops 1 | bytes 8 | tf_op jit(solution)/shard_map/psum | solution.py:168
  1157.2 16.1 %all_gather.67 = f32[1,64,2,16]{3,2,0,1:T(2,128)S(1)} all-gather(f32[1,4,2,16]{3,2,0,1:T(2,128)S(1)} %copy.243), channel_id=1, replica_groups=mesh['by'=8,'bx'=16] {'bx'}, dimensions={1}, use_global_device_ids=true | all-gather | bytes 8704 | tf_op jit(solution)/shard_map/all_gather | solution.py:126
  1173.6 17.5 %all_gather.66 = f32[1,64,2,128]{3,2,0,1:T(2,128)S(1)} all-gather(f32[1,4,2,128]{3,2,0,1:T(2,128)S(1)} %maximum_bitcast_fusion.13), channel_id=1, replica_groups=mesh['by'=8,'bx'=16] {'bx'}, dimensions={1}, use_global_device_ids=true | all-gather | bytes 69632 | tf_op jit(solution)/shard_map/all_gather | solution.py:127
  1191.3 12.6 collective-permute-start.14
  1204.3 2.7 collective-permute-start.15
  1207.2 2.3 collective-permute-done.15
  1210.7 5.4 broadcast.122
  1216.1 43.3 %while.35 = (s32[]{:T(128)}, f32[4,16,2048]{2,1,0:T(8,128)S(1)}, f32[20,4,16,2048]{3,2,1,0:T(8,128)}, f32[20,4,16,2048]{3,2,1,0:T(8,128)}, f32[20,4,2048]{2,1,0:T(4,128)S(1)}, /*index=5*/s32[]{:T(128)}, s32[]{:T(128)}, s32[]{:T(128)}) while((s32[]{:T(128)}, f32[4,16,2048]{2,1,0:T(8,128)S(1)}, f32[20,4,16,2048]{3,2,1,0:T(8,128)}, ...), condition=%wide.region_3.4_spmd.clone, body=%wide.region_2.3_spmd.clone.sunk | while | flops 393220 | bytes 2195571 | solution.py:66
  1216.1 2.2 bitcast_dynamic-update-slice_fusion.8
  1218.3 2.2 bitcast_dynamic-update-slice_fusion.8
  1220.4 2.2 bitcast_dynamic-update-slice_fusion.8
  1224.8 2.2 bitcast_dynamic-update-slice_fusion.8
  1226.9 2.2 bitcast_dynamic-update-slice_fusion.8
  1229.1 2.2 bitcast_dynamic-update-slice_fusion.8
  1231.3 2.2 bitcast_dynamic-update-slice_fusion.8
  1233.4 2.2 bitcast_dynamic-update-slice_fusion.8
  1235.6 2.2 bitcast_dynamic-update-slice_fusion.8
  1259.4 64.3 %psum.95 = f32[]{:T(128)} all-reduce(f32[]{:T(128)} %fusion.39), channel_id=1, replica_groups=mesh['by'=8,'bx'=16] {'by','bx'}, use_global_device_ids=true, to_apply=%region_28.29 | all-reduce | flops 1 | bytes 8 | tf_op jit(solution)/shard_map/psum | solution.py:174
  (290 shorter events, 120.6 us)
Async XLA Ops:
  7.2 112.6 %all-gather.2.cloned.1.call-start = ((), (), s32[]{:S(2)}) async-start(), calls=%async_computation | async-start | bytes 2228224 | tf_op jit(solution)/shard_map/all_gather | solution.py:107
  16.1 3.8 slice-start
  29.7 9.2 copy-start.1
  54.4 65.2 %copy-start = (s32[4,16,128]{2,1,0:T(8,128)S(1)}, s32[4,16,128]{2,1,0:T(8,128)}, u32[]{:S(2)}) copy-start(s32[4,16,128]{2,1,0:T(8,128)} %param.21) | copy-start | bytes 98308
  160.6 68.4 %collective-permute-start.2 = (f32[1,1,64,128]{3,2,0,1:T(8,128)S(1)}, f32[1,1,64,128]{3,2,0,1:T(8,128)S(1)}, u32[]{:S(2)}, u32[]{:S(2)}) collective-permute-start(f32[1,1,64,128]{3,2,0,1:T(8,128)S(1)} %get-tuple-element.331), channel_id=1, source_target_pairs={{0,16},{16,32},{32,48},{48,64},{64,80},{80,96},{96,112},{1,17},{17... | collective-permute-start | bytes 98312 | tf_op jit(solution)/shard_map/ppermute | solution.py:20
  175.2 54.1 %collective-permute-start.3 = (f32[1,1,64,128]{3,2,0,1:T(8,128)S(1)}, f32[1,1,64,128]{3,2,0,1:T(8,128)S(1)}, u32[]{:S(2)}, u32[]{:S(2)}) collective-permute-start(f32[1,1,64,128]{3,2,0,1:T(8,128)S(1)} %get-tuple-element.332), channel_id=1, source_target_pairs={{16,0},{32,16},{48,32},{64,48},{80,64},{96,80},{112,96},{17,1},{33... | collective-permute-start | bytes 98312 | tf_op jit(solution)/shard_map/ppermute | solution.py:23
  212.5 17.2 %collective-permute-start = (f32[1,2,64,128]{3,2,0,1:T(8,128)S(1)}, f32[1,2,64,128]{3,2,0,1:T(8,128)S(1)}, u32[]{:S(2)}, u32[]{:S(2)}) collective-permute-start(f32[1,2,64,128]{3,2,0,1:T(8,128)S(1)} %get-tuple-element.298), channel_id=1, source_target_pairs={{0,16},{16,32},{32,48},{48,64},{64,80},{80,96},{96,112},{1,17},{17... | collective-permute-start | bytes 196616 | tf_op jit(solution)/shard_map/ppermute | solution.py:20
  227.1 5.6 collective-permute-start.1
  267.7 15.3 %collective-permute-start.4 = (f32[1,1,64,128]{3,2,0,1:T(8,128)S(1)}, f32[1,1,64,128]{3,2,0,1:T(8,128)S(1)}, u32[]{:S(2)}, u32[]{:S(2)}) collective-permute-start(f32[1,1,64,128]{3,2,0,1:T(8,128)S(1)} %get-tuple-element.325), channel_id=1, source_target_pairs={{0,16},{16,32},{32,48},{48,64},{64,80},{80,96},{96,112},{1,17},{17... | collective-permute-start | bytes 98312 | tf_op jit(solution)/shard_map/ppermute | solution.py:20
  281.0 5.2 collective-permute-start.5
  452.1 15.9 %collective-permute-start.6 = (f32[1,1,64,128]{3,2,0,1:T(8,128)S(1)}, f32[1,1,64,128]{3,2,0,1:T(8,128)S(1)}, u32[]{:S(2)}, u32[]{:S(2)}) collective-permute-start(f32[1,1,64,128]{3,2,0,1:T(8,128)S(1)} %get-tuple-element.321), channel_id=1, source_target_pairs={{0,16},{16,32},{32,48},{48,64},{64,80},{80,96},{96,112},{1,17},{17... | collective-permute-start | bytes 98312 | tf_op jit(solution)/shard_map/ppermute | solution.py:20
  466.0 5.2 collective-permute-start.7
  635.9 17.5 %collective-permute-start.8 = (f32[1,1,64,128]{3,2,0,1:T(8,128)S(1)}, f32[1,1,64,128]{3,2,0,1:T(8,128)S(1)}, u32[]{:S(2)}, u32[]{:S(2)}) collective-permute-start(f32[1,1,64,128]{3,2,0,1:T(8,128)S(1)} %get-tuple-element.317), channel_id=1, source_target_pairs={{0,16},{16,32},{32,48},{48,64},{64,80},{80,96},{96,112},{1,17},{17... | collective-permute-start | bytes 98312 | tf_op jit(solution)/shard_map/ppermute | solution.py:20
  651.5 5.2 collective-permute-start.9
  821.6 15.7 %collective-permute-start.10 = (f32[1,1,64,128]{3,2,0,1:T(8,128)S(1)}, f32[1,1,64,128]{3,2,0,1:T(8,128)S(1)}, u32[]{:S(2)}, u32[]{:S(2)}) collective-permute-start(f32[1,1,64,128]{3,2,0,1:T(8,128)S(1)} %get-tuple-element.313), channel_id=1, source_target_pairs={{0,16},{16,32},{32,48},{48,64},{64,80},{80,96},{96,112},{1,17},{17... | collective-permute-start | bytes 98312 | tf_op jit(solution)/shard_map/ppermute | solution.py:20
  834.7 5.2 collective-permute-start.11
  1005.6 17.4 %collective-permute-start.12 = (f32[1,1,64,128]{3,2,0,1:T(8,128)S(1)}, f32[1,1,64,128]{3,2,0,1:T(8,128)S(1)}, u32[]{:S(2)}, u32[]{:S(2)}) collective-permute-start(f32[1,1,64,128]{3,2,0,1:T(8,128)S(1)} %get-tuple-element.309), channel_id=1, source_target_pairs={{0,16},{16,32},{32,48},{48,64},{64,80},{80,96},{96,112},{1,17},{17... | collective-permute-start | bytes 98312 | tf_op jit(solution)/shard_map/ppermute | solution.py:20
  1021.0 5.2 collective-permute-start.13
  1191.3 15.7 %collective-permute-start.14 = (f32[1,1,64,128]{3,2,0,1:T(8,128)S(1)}, f32[1,1,64,128]{3,2,0,1:T(8,128)S(1)}, u32[]{:S(2)}, u32[]{:S(2)}) collective-permute-start(f32[1,1,64,128]{3,2,0,1:T(8,128)S(1)} %get-tuple-element.305), channel_id=1, source_target_pairs={{0,16},{16,32},{32,48},{48,64},{64,80},{80,96},{96,112},{1,17},{17... | collective-permute-start | bytes 98312 | tf_op jit(solution)/shard_map/ppermute | solution.py:20
  1204.3 5.2 collective-permute-start.15
Sparse Core Ops, SparseCore 0:
  15.3 46.3 all-gather.1
where the time goes:
time: 1340 us; the launch traced here: 1330 us
  blocking collectives  969 us (72%)
  other arithmetic  146 us (11%)
  starting transfers between devices  128 us (10%)
  local copies, waits for them, and re-layouts  29.9 us (2%)
  between operations  29.7 us (2%)
  waiting for transfers between devices  19.4 us (1%)
    psum x6, blocking collectives, weighted(): return lax.psum(jnp.sum(residual_now * precond_now), ('by', 'bx'))  381 us
    psum x5, blocking collectives, local(): lax.psum(jnp.sum(direction * image_field), ('by', 'bx'))  317 us
    all_gather x8, blocking collectives, extend(): lax.all_gather(edge_rows, 'bx', axis=1, tiled=True)  137 us
    all_gather x8, blocking collectives, extend(): lax.all_gather(edge_cols, 'bx', axis=1, tiled=True)  135 us
    ppermute x8, starting transfers between devices, padded_2(): lax.ppermute(lax.slice_in_dim(block, block.shape[dim] - width, None, axis...  111 us
    dynamic_update_slice x60, other arithmetic, column_step(): lax.scan(forward, start_carry, (-mixing_above, diagonal, -mixing, right_s...  101 us
  transfers between devices with their start and end apart: 17, of which 7 were waited for; matrix products, arithmetic and copies ran while one was open for 8% of the time, Pallas kernels for 0%

commit v1 on v0

v1 whole, which is shorter than its diff:
```python
import jax
import jax.numpy as jnp
from jax import lax
from jax.experimental import pallas as pl
from jax.experimental.pallas import tpu as pltpu
from jax.sharding import PartitionSpec as P

MESH = pl.DeviceIdType.MESH
ITERS = 6
RESTORE = 0.5
SURFACE = 0.1
FACE_SCALE = 2.0
LEV, TR, BH, BW = 20, 16, 16, 128
GBX, BLOCKS, NBX, NBY = 64, 4, 16, 8
LANES = 256
FACE = FACE_SCALE / LEV
SHIFTS = (0.0, 2.0, 1.0, 1.577, 0.4226, 0.1)
ALPHA_MAX = 82.0
PAIRS = [(i, j) for i in range(ITERS) for j in range(i, ITERS + 1)]


def columns_kernel(tr_ref, speed_ref, diff_ref, wet_ref, patch_ref, out_ref, coef):
    lanes = tr_ref.shape[3]
    wet = wet_ref[...]
    zero = jnp.zeros(wet.shape, jnp.float32)
    mix_above, pos_above, neg_above, ratio_above = zero, zero, zero, zero
    for k in range(LEV):
        is_wet = (wet > k).astype(jnp.float32)
        is_open = (wet > k + 1).astype(jnp.float32)
        speed = speed_ref[k] * is_open
        pos, neg = jnp.maximum(speed, 0.0), jnp.minimum(speed, 0.0)
        mix = diff_ref[k] * is_open
        pivot = 1.0 + mix + mix_above
        if k == 0:
            pivot = pivot + RESTORE * is_wet
        pivot = pivot - mix_above * ratio_above
        inv = 1.0 / pivot
        scale = is_wet * inv
        coef[0, k] = scale * (1.0 + neg - pos_above)
        coef[1, k] = scale * pos
        coef[2, k] = -scale * neg_above
        coef[3, k] = mix_above * inv
        ratio = mix * inv
        coef[4, k] = ratio
        if k == 0:
            coef[5, 0] = RESTORE * scale
        mix_above, pos_above, neg_above, ratio_above = mix, pos, neg, ratio
    ids = lax.broadcasted_iota(jnp.int32, (TR, 128), 0)
    for n in range(BLOCKS):
        for l in range(lanes // 128):
            sl = pl.ds(l * 128, 128)

            def c(i, k):
                return coef[i, k, pl.ds(n, 1), sl]

            values = []
            above, here, value = None, tr_ref[0, n, :, sl], None
            for k in range(LEV):
                new = c(0, k) * here
                if k + 1 < LEV:
                    below = tr_ref[k + 1, n, :, sl]
                    new = new + c(1, k) * below
                if k == 0:
                    target = patch_ref[pl.ds(n, 1), sl] == ids
                    new = new + jnp.where(target, c(5, 0), 0.0)
                else:
                    new = new + c(2, k) * above + c(3, k) * value
                value = new
                values.append(value)
                above, here = here, below
            follow = values[-1]
            out_ref[LEV - 1, n, :, sl] = follow
            for k in range(LEV - 2, -1, -1):
                follow = values[k] + c(4, k) * follow
                out_ref[k, n, :, sl] = follow


def column_step(tracers, speed, diff, wet, patch):
    lanes = 256
    cells = wet.shape[1]
    big = pl.BlockSpec((LEV, BLOCKS, TR, lanes), lambda i: (0, 0, 0, i))
    mid = pl.BlockSpec((LEV, BLOCKS, lanes), lambda i: (0, 0, i))
    low = pl.BlockSpec((BLOCKS, lanes), lambda i: (0, i))
    return pl.pallas_call(
        columns_kernel,
        grid=(cells // lanes,),
        in_specs=[big, mid, mid, low, low],
        out_specs=big,
        out_shape=jax.ShapeDtypeStruct(tracers.shape, jnp.float32),
        scratch_shapes=[pltpu.VMEM((6, LEV, BLOCKS, lanes), jnp.float32)],
        compiler_params=pltpu.CompilerParams(dimension_semantics=("arbitrary",)),
        name="columns",
    )(tracers, speed, diff, wet, patch)


def table_index(kind, role, slot, side):
    return ((kind * 3 + role) * BLOCKS + slot) * 3 + side


def barotropic_kernel(
    tab, buoy_ref, wet_ref, prior_ref, land_ref, out_ref,
    gat, nsend, nrecv, basis, gram, ring_a, ring_b, ssem, rsem,
):
    row = lax.axis_index("by")
    me = lax.axis_index("bx")
    core = lax.rem(row, 2)
    step_a = 4 - 3 * core
    step_b = 1 + 3 * core
    px, py = me // 4, lax.rem(me, 4)
    a = px + core * (py - px)
    b = py + core * (px - py)

    def dev(i, j):
        return lax.rem(a + i, 4) * step_a + lax.rem(b + j, 4) * step_b

    barrier = pltpu.get_barrier_semaphore()
    for i in range(1, NBX):
        pl.semaphore_signal(
            barrier, inc=1, device_id={"bx": lax.rem(me + i, NBX)}, device_id_type=MESH
        )
    for i in range(1, NBY):
        pl.semaphore_signal(
            barrier, inc=1, device_id={"by": lax.rem(row + i, NBY)}, device_id_type=MESH
        )

    mine = me * BLOCKS
    wet = wet_ref[...]
    total = jnp.zeros(wet.shape, jnp.float32)
    for k in range(LEV):
        total = total + jnp.where(wet > k, buoy_ref[k].astype(jnp.float32), 0.0)
    fields = (total, wet.astype(jnp.float32), prior_ref[...])
    for q in range(3):
        for n in range(BLOCKS):
            for r in range(BH):
                gat[mine + n, q, pl.ds(r, 1), :] = fields[q][n : n + 1, r * BW : (r + 1) * BW]
    for n in range(BLOCKS):
        gat[mine + n, 3] = land_ref[n].astype(jnp.float32)

    pl.semaphore_wait(barrier, NBX - 1 + NBY - 1)

    copies = {}

    def send(tag, where, start, count, to):
        piece = gat.at[pl.ds(where * BLOCKS + start, count)]
        copies[tag] = pltpu.make_async_remote_copy(
            src_ref=piece,
            dst_ref=piece,
            send_sem=ssem.at[tag],
            recv_sem=rsem.at[tag],
            device_id={"bx": to},
            device_id_type=MESH,
        )
        copies[tag].start()

    def arrived(tag):
        copies[tag].wait_recv()

    half = BLOCKS // 2
    send(0, me, 0, BLOCKS, dev(1, 0))
    send(1, me, 0, BLOCKS, dev(3, 0))
    send(4, me, 0, BLOCKS, dev(0, 1))
    send(5, me, 0, BLOCKS, dev(0, 3))
    arrived(0)
    send(2, dev(3, 0), 0, half, dev(1, 0))
    send(8, dev(3, 0), 0, BLOCKS, dev(0, 1))
    send(9, dev(3, 0), 0, BLOCKS, dev(0, 3))
    arrived(1)
    send(3, dev(1, 0), half, half, dev(3, 0))
    send(12, dev(1, 0), 0, BLOCKS, dev(0, 1))
    send(13, dev(1, 0), 0, BLOCKS, dev(0, 3))

    def relay(t, i):
        arrived(4 + 4 * t)
        send(6 + 4 * t, dev(i, 3), 0, half, dev(0, 1))
        arrived(5 + 4 * t)
        send(7 + 4 * t, dev(i, 1), half, half, dev(0, 3))

    relay(0, 0)
    arrived(2)
    arrived(3)
    send(16, dev(2, 0), 0, BLOCKS, dev(0, 1))
    send(17, dev(2, 0), 0, BLOCKS, dev(0, 3))
    relay(1, 3)
    relay(2, 1)
    relay(3, 2)
    for t in range(4):
        arrived(6 + 4 * t)
        arrived(7 + 4 * t)
    for tag in range(20):
        copies[tag].wait_send()

    west_half = lax.broadcasted_iota(jnp.int32, (8, BW), 1) >= BW // 2

    def piece(role, n, q, side, rows):
        kind = 1 if q == 3 else 0
        return gat[tab[table_index(kind, role, n, side)], q, rows, :]

    def extended(role, n, q, rows):
        middle = piece(role, n, q, 1, rows)
        beside = jnp.where(west_half, piece(role, n, q, 0, rows), piece(role, n, q, 2, rows))
        return middle, beside

    for role, rows in ((1, pl.ds(BH - 8, 8)), (2, pl.ds(0, 8))):
        for n in range(BLOCKS):
            for q in range(4):
                middle, beside = extended(role, n, q, rows)
                nsend[role - 1, n, q, :, pl.ds(0, BW)] = middle
                nsend[role - 1, n, q, :, pl.ds(BW, BW)] = beside
    halo = []
    for d in range(2):
        to = lax.rem(row + (1 if d == 0 else NBY - 1), NBY)
        copy = pltpu.make_async_remote_copy(
            src_ref=nsend.at[d],
            dst_ref=nrecv.at[d],
            send_sem=ssem.at[20 + d],
            recv_sem=rsem.at[20 + d],
            device_id={"by": to},
            device_id_type=MESH,
        )
        copy.start()
        halo.append(copy)
    for copy in halo:
        copy.wait()

    has_north = (row > 0).astype(jnp.float32)
    has_south = (row < NBY - 1).astype(jnp.float32)
    acc = [None] * len(PAIRS)
    for n in range(BLOCKS):
        whole = []
        for q in range(4):
            north, south = nrecv[0, n, q], nrecv[1, n, q]
            if q == 3:
                north, south = north * has_north, south * has_south
            parts = [north]
            for r in range(0, BH, 8):
                middle, beside = extended(0, n, q, pl.ds(r, 8))
                parts.append(jnp.concatenate([middle, beside], axis=1))
            parts.append(south)
            whole.append(jnp.concatenate(parts, axis=0))
        force, depth, prior, ocean = whole
        rows = BH + 16

        def east(v):
            return pltpu.roll(v, LANES - 1, 1)

        def west(v):
            return pltpu.roll(v, 1, 1)

        def south_of(v):
            return pltpu.roll(v, rows - 1, 0)

        def north_of(v):
            return pltpu.roll(v, 1, 0)

        face_e = FACE * jnp.minimum(depth, east(depth)) * ocean * east(ocean)
        face_s = FACE * jnp.minimum(depth, south_of(depth)) * ocean * south_of(ocean)
        face_w, face_n = west(face_e), north_of(face_s)
        centre = SURFACE * ocean + (1.0 - ocean)
        diag = centre + face_e + face_w + face_s + face_n
        inv = 1.0 / diag
        centre, face_e, face_w = centre * inv, face_e * inv, face_w * inv
        face_s, face_n = face_s * inv, face_n * inv

        def scaled(v):
            out = centre * v + face_e * (v - east(v)) + face_w * (v - west(v))
            return out + face_s * (v - south_of(v)) + face_n * (v - north_of(v))

        def own(v):
            return v[8 : 8 + BH, :BW]

        guess = ocean * prior
        u = ocean * force * inv - scaled(guess)
        weight = own(diag)
        basis[n, ITERS] = own(guess)
        mine_of, weighted = [], []
        for k in range(ITERS + 1):
            mine_of.append(own(u))
            if k < ITERS:
                basis[n, k] = mine_of[k]
                weighted.append(weight * mine_of[k])
                image = scaled(u)
                u = image - SHIFTS[k] * u if SHIFTS[k] else image
        for e, (i, j) in enumerate(PAIRS):
            prod = weighted[i] * mine_of[j]
            prod = prod[:8] + prod[8:]
            acc[e] = prod if acc[e] is None else acc[e] + prod

    entries = 32
    for e in range(len(PAIRS)):
        gram[pl.ds(e, 1), :] = jnp.sum(acc[e], axis=0, keepdims=True)
    gram[pl.ds(len(PAIRS), entries - len(PAIRS)), :] = jnp.zeros(
        (entries - len(PAIRS), BW), jnp.float32
    )
    on_diag = lax.broadcasted_iota(jnp.int32, (entries, BW), 0) == lax.broadcasted_iota(
        jnp.int32, (entries, BW), 1
    )
    placed = jnp.where(on_diag, jnp.sum(gram[...], axis=1, keepdims=True), 0.0)
    packed = placed[0:8] + placed[8:16] + placed[16:24] + placed[24:32]

    def all_sum(value, ring, index, count, axis, base):
        ring[index] = value
        sent = []
        for i in range(1, count):
            copy = pltpu.make_async_remote_copy(
                src_ref=ring.at[index],
                dst_ref=ring.at[index],
                send_sem=ssem.at[base + i],
                recv_sem=rsem.at[base + i],
                device_id={axis: lax.rem(index + i, count)},
                device_id_type=MESH,
            )
            copy.start()
            sent.append(copy)
        for copy in sent:
            copy.wait()
        return jnp.sum(ring[...], axis=0)

    packed = all_sum(packed, ring_a, me, NBX, "bx", 22)
    packed = all_sum(packed, ring_b, row, NBY, "by", 22 + NBX)
    line = jnp.sum(packed, axis=0, keepdims=True)
    spread = jnp.sum(jnp.where(on_diag, line, 0.0), axis=1, keepdims=True)
    spread = jnp.broadcast_to(spread, (entries, BW))
    g = {}
    for e, (i, j) in enumerate(PAIRS):
        g[i, j] = g[j, i] = spread[e : e + 1]

    def form(left, right):
        out = None
        for i, vi in enumerate(left):
            inner = None
            for j, vj in enumerate(right):
                term = g[i, j] * vj
                inner = term if inner is None else inner + term
            out = vi * inner if out is None else out + vi * inner
        return out

    one = jnp.ones((1, BW), jnp.float32)
    zero = jnp.zeros((1, BW), jnp.float32)
    p, z = [one], [one]
    x = [zero] * ITERS
    rz = g[0, 0]
    for it in range(ITERS):
        y = [SHIFTS[k] * p[k] if SHIFTS[k] else zero for k in range(it + 1)] + [zero]
        for k in range(it + 1):
            y[k + 1] = y[k + 1] + p[k]
        pq = form(p, y)
        live = jnp.logical_and(rz > 0.0, pq > 0.0)
        alpha = jnp.where(live, rz, 0.0) / jnp.where(live, pq, 1.0)
        alpha = jnp.minimum(alpha, ALPHA_MAX)
        for k in range(it + 1):
            x[k] = x[k] + alpha * p[k]
        if it + 1 < ITERS:
            z = [zk - alpha * yk for zk, yk in zip(z + [zero], y)]
            rz_new = jnp.maximum(form(z, z), 0.0)
            beta = jnp.where(live, rz_new, 0.0) / jnp.where(live, rz, 1.0)
            p = [zk + beta * pk for zk, pk in zip(z, p + [zero])]
            rz = rz_new
    for n in range(BLOCKS):
        height = basis[n, ITERS]
        for k in range(ITERS):
            height = height + x[k] * basis[n, k]
        out_ref[n] = height


def barotropic(table, buoyancy, wet, prior, land):
    vmem = pl.BlockSpec(memory_space=pltpu.VMEM)
    tags = 22 + NBX + NBY
    return pl.pallas_call(
        barotropic_kernel,
        out_shape=jax.ShapeDtypeStruct((BLOCKS, BH, BW), jnp.float32),
        in_specs=[pl.BlockSpec(memory_space=pltpu.SMEM)] + [vmem] * 4,
        out_specs=vmem,
        scratch_shapes=[
            pltpu.VMEM((GBX, 4, BH, BW), jnp.float32),
            pltpu.VMEM((2, BLOCKS, 4, 8, LANES), jnp.float32),
            pltpu.VMEM((2, BLOCKS, 4, 8, LANES), jnp.float32),
            pltpu.VMEM((BLOCKS, ITERS + 1, BH, BW), jnp.float32),
            pltpu.VMEM((32, BW), jnp.float32),
            pltpu.VMEM((NBX, 8, BW), jnp.float32),
            pltpu.VMEM((NBY, 8, BW), jnp.float32),
            pltpu.SemaphoreType.DMA((tags,)),
            pltpu.SemaphoreType.DMA((tags,)),
        ],
        compiler_params=pltpu.CompilerParams(collective_id=0, has_side_effects=True),
        name="barotropic",
    )(table, buoyancy, wet, prior, land)


def index_table(baroclinic_map, barotropic_map):
    row, column = lax.axis_index("by"), lax.axis_index("bx")
    first = row * GBX
    clinic = lax.dynamic_slice_in_dim(baroclinic_map, first, GBX) - first
    tropic = lax.dynamic_slice_in_dim(barotropic_map, first, GBX) - first
    rows = (row + jnp.array([0, 1, NBY - 1], jnp.int32)) % NBY
    blocks = barotropic_map.reshape(NBY, NBX, BLOCKS)
    wanted = jnp.stack(
        [lax.dynamic_slice(blocks, (rows[i], column, 0), (1, 1, BLOCKS))[0, 0] for i in range(3)]
    ) % GBX
    sides = jnp.array([-1, 0, 1], jnp.int32)
    wanted = (wanted[:, :, None] + sides + GBX) % GBX
    places = jnp.arange(GBX, dtype=jnp.int32)
    held = jnp.stack([clinic, tropic])
    match = held[:, None, None, None, :] == wanted[None, :, :, :, None]
    return jnp.sum(jnp.where(match, places, 0), axis=-1).reshape(-1)


def local(
    tracers, vertical_speed, diffusivity, buoyancy_force, wet_levels, surface_patch,
    prior_height, land_mask, baroclinic_map, barotropic_map,
):
    table = index_table(baroclinic_map, barotropic_map)
    height = barotropic(table, buoyancy_force, wet_levels, prior_height, land_mask)
    new_tracers = column_step(tracers, vertical_speed, diffusivity, wet_levels, surface_patch)
    return new_tracers, height


def solution(mesh):
    return jax.shard_map(
        local,
        mesh=mesh,
        in_specs=(
            P(None, ("by", "bx"), None, None),
            P(None, ("by", "bx"), None),
            P(None, ("by", "bx"), None),
            P(None, ("by", "bx"), None),
            P(("by", "bx"), None),
            P(("by", "bx"), None),
            P(("by", "bx"), None),
            P(("by", "bx"), None, None),
            P(),
            P(),
        ),
        out_specs=(P(None, ("by", "bx"), None, None), P(("by", "bx"), None, None)),
        check_vma=False,
    )
```

time: 1340 us -> 65.6 us (0.05)
  blocking collectives: 969 us -> 0 us
  other arithmetic: 146 us -> 2.67 us
  starting transfers between devices: 128 us -> 0 us
  Pallas kernels: 0 us -> 53.3 us
  local copies, waits for them, and re-layouts: 29.9 us -> 2.79 us
  between operations: 29.7 us -> 6.46 us
  waiting for transfers between devices: 19.4 us -> 0 us
    psum x11 -> x0, blocking collectives: 697 us -> none  [the longest x6 381 us: weighted(): return lax.psum(jnp.sum(residual_now * precond_now), ('by', 'bx'))]
    all_gather x16 -> x0, blocking collectives: 272 us -> none  [the longest x8 137 us: extend(): lax.all_gather(edge_rows, 'bx', axis=1, tiled=True)]
    ppermute x16 -> x0, starting transfers between devices: 128 us -> none  [the longest x8 111 us: padded_2(): lax.ppermute(lax.slice_in_dim(block, block.shape[dim] - width, None, axis...]
    dynamic_update_slice x60 -> x0, other arithmetic: 101 us -> none  [column_step(): lax.scan(forward, start_carry, (-mixing_above, diagonal, -mixing, right_s...]
    pallas_call x0 -> x2, Pallas kernels: none -> 53.3 us  [the longest x1 41 us: barotropic(): pl.pallas_call(barotropic_kernel, out_shape=jax.ShapeDtypeStruct((BLOCKS,...]
    add x8 -> x0, other arithmetic: 26 us -> none  [the longest x1 15.5 us: column_step(): right_side = advected + surface_row[:, :, None] * targets[None]]
    ppermute x16 -> x0, waiting for transfers between devices: 19.4 us -> none  [the longest x8 19.4 us: padded_2(): lax.ppermute(lax.slice_in_dim(block, 0, width, axis=dim), axis, backward)]
    slice x36 -> x1, local copies, waits for them, and re-layouts: 14.9 us -> 0.61 us  [index_table(): rows[i]]
  transfers between devices with their start and end apart: 17 -> 0, of which waited for: 7 -> 0; matrix products, arithmetic and copies ran while one was open for 8% -> 0% of each run, Pallas kernels for 0% -> 0%
where the time goes in v1:
time: 65.6 us; the launch traced here: 65.2 us
  Pallas kernels  53.3 us (81%)
  between operations  6.46 us (10%)
  local copies, waits for them, and re-layouts  2.79 us (4%)
  other arithmetic  2.67 us (4%)
    pallas_call x1, Pallas kernels, barotropic(): pl.pallas_call(barotropic_kernel, out_shape=jax.ShapeDtypeStruct((BLOCKS,...  41 us
    pallas_call x1, Pallas kernels, column_step(): pl.pallas_call(columns_kernel, grid=(cells // lanes,), in_specs=[big, mid...  12.2 us

profile of v1, /device:TPU:1, one launch (start us, length us, event | category | flops | bytes accessed | tf_op | source)
XLA Modules:
  0.0 65.2 jit_solution(5836860430964710791)
XLA Ops:
  0.6 0.7 %and_select_fusion = s32[3]{0:T(128)S(1)} fusion(s32[3]{0:T(128)} %constant.56.clone, s32[]{:T(128)S(6)} %axis_index.23), kind=kLoop, calls=%fused_computation.11 | loop fusion | flops 36 | bytes 28 | tf_op jit(solution)/shard_map/jit(remainder)/select_n | solution.py:394
  1.3 0.8 %subtract_bitcast_fusion = (s32[1,64]{1,0:T(1,128)S(1)}, s32[1,64]{1,0:T(1,128)S(1)}) fusion(s32[512]{0:T(512)} %param.21, s32[]{:T(128)S(6)} %select_n.49, s32[]{:T(128)S(6)} %mul.3, s32[512]{0:T(512)} %param.20), kind=kLoop, calls=%fused_computation.20 | loop fusion | flops 128 | bytes 1032 | tf_op jit(solution)/shard_map/stack | solution.py:402
  2.1 0.6 fusion.6
  8.5 0.8 %reshape.96 = s32[8,16,4]{2,1,0:T(8,128)S(1)} reshape(s32[512]{0:T(512)} %param.21) | data formatting | bytes 4096 | tf_op jit(solution)/shard_map/reshape | solution.py:395
  9.3 0.7 %add_select_fusion = s32[3,4,3]{1,2,0:T(4,128)S(1)} fusion(s32[3]{0:T(128)} %constant.57.clone, s32[3,4]{1,0:T(4,128)S(1)} %add_select_fusion.1), kind=kLoop, calls=%fused_computation.1 | loop fusion | flops 468 | bytes 204 | tf_op jit(solution)/shard_map/jit(remainder)/select_n | solution.py:400
  10.1 0.5 select_reduce_fusion
  10.5 0.1 copy.14
  10.7 0.6 reshape.97.tab
  11.3 41.0 %barotropic.1 = f32[4,16,128]{2,1,0:T(8,128)} custom-call(s32[72]{0:T(128)} %reshape.97.tab, bf16[20,4,2048]{2,1,0:T(4,128)(2,1)} %buoy_ref.1, s32[4,2048]{1,0:T(4,128)} %wet_ref.3, f32[4,2048]{1,0:T(4,128)} %prior_ref.1, s32[4,16,128]{2,1,0:T(8,128)} %land_ref.1), custom_call_target="tpu_custom_call" | custom-call | tf_op jit(solution)/shard_map/barotropic/pallas_call | solution.py:368
  52.3 0.0 copy-start
  52.3 12.2 %columns.1 = f32[20,4,16,2048]{3,2,1,0:T(8,128)} custom-call(f32[20,4,16,2048]{3,2,1,0:T(8,128)} %tr_ref.1, f32[20,4,2048]{2,1,0:T(4,128)} %speed_ref.1, f32[20,4,2048]{2,1,0:T(4,128)} %diff_ref.1, s32[4,2048]{1,0:T(4,128)} %wet_ref.3, s32[4,2048]{1,0:T(4,128)} %patch_ref.1), custom_call_target="tpu_custom_call" | custom-call | tf_op jit(solution)/shard_map/columns/pallas_call | solution.py:84
  64.6 0.0 copy-done
  64.6 0.6 copy.16
  (3 shorter events, 0.0 us)
Async XLA Ops:
  52.3 12.2 %copy-start = (f32[4,16,128]{2,1,0:T(8,128)S(1)}, f32[4,16,128]{2,1,0:T(8,128)}, u32[]{:S(2)}) copy-start(f32[4,16,128]{2,1,0:T(8,128)} %barotropic.1) | copy-start | bytes 98308

commit v2 on v1

v2 whole, which is shorter than its diff:
```python
import jax
import jax.numpy as jnp
from jax import lax
from jax.experimental import pallas as pl
from jax.experimental.pallas import tpu as pltpu
from jax.sharding import PartitionSpec as P

MESH = pl.DeviceIdType.MESH
ITERS = 6
RESTORE = 0.5
SURFACE = 0.1
FACE_SCALE = 2.0
LEV, TR, BH, BW = 20, 16, 16, 128
CELLS = BH * BW
GBX, BLOCKS, NBX, NBY = 64, 4, 16, 8
LANES = 256
FACE = FACE_SCALE / LEV
SHIFTS = (0.0, 2.0, 1.0, 1.577, 0.4226, 0.1)
ALPHA_MAX = 82.0
PAIRS = [(i, j) for i in range(ITERS) for j in range(i, ITERS + 1)]
ENTRIES = 32
CHUNKS = 8
PARTS = (range(0, 2), range(2, 5), range(5, 8))
OWN_TILES = BLOCKS * 3 * 2 + 4
ROW_TILES = BLOCKS * 4 + 2


def columns(tile, tr, speed_ref, diff_ref, wet_ref, patch_ref, coef):
    sl = pl.ds(pl.multiple_of(tile * 128, 128), 128)
    wet = wet_ref[:, sl]
    zero = jnp.zeros(wet.shape, jnp.float32)
    mix_above, pos_above, neg_above, ratio_above = zero, zero, zero, zero
    for k in range(LEV):
        is_wet = (wet > k).astype(jnp.float32)
        is_open = (wet > k + 1).astype(jnp.float32)
        speed = speed_ref[k, :, sl] * is_open
        pos, neg = jnp.maximum(speed, 0.0), jnp.minimum(speed, 0.0)
        mix = diff_ref[k, :, sl] * is_open
        pivot = 1.0 + mix + mix_above
        if k == 0:
            pivot = pivot + RESTORE * is_wet
        pivot = pivot - mix_above * ratio_above
        inv = 1.0 / pivot
        scale = is_wet * inv
        coef[0, k] = scale * (1.0 + neg - pos_above)
        coef[1, k] = scale * pos
        coef[2, k] = -scale * neg_above
        coef[3, k] = mix_above * inv
        ratio = mix * inv
        coef[4, k] = ratio
        if k == 0:
            coef[5, 0] = RESTORE * scale
        mix_above, pos_above, neg_above, ratio_above = mix, pos, neg, ratio
    ids = lax.broadcasted_iota(jnp.int32, (TR, 128), 0)
    for n in range(BLOCKS):

        def c(i, k):
            return coef[i, k, pl.ds(n, 1), :]

        values = []
        above, here, value = None, tr[0, n, :, sl], None
        for k in range(LEV):
            new = c(0, k) * here
            if k + 1 < LEV:
                below = tr[k + 1, n, :, sl]
                new = new + c(1, k) * below
            if k == 0:
                target = patch_ref[pl.ds(n, 1), sl] == ids
                new = new + jnp.where(target, c(5, 0), 0.0)
            else:
                new = new + c(2, k) * above + c(3, k) * value
            value = new
            values.append(value)
            above, here = here, below
        follow = values[-1]
        tr[LEV - 1, n, :, sl] = follow
        for k in range(LEV - 2, -1, -1):
            follow = values[k] + c(4, k) * follow
            tr[k, n, :, sl] = follow


def step_kernel(
    cmap_hbm, tmap_hbm, buoy_hbm, wet_hbm, patch_hbm, prior_hbm, land_hbm, speed_hbm, diff_hbm, tr_hbm,
    tr, out_ref,
    cmap, tmap, buoy_ref, wet_ref, patch_ref, prior_ref, land_ref, speed_ref, diff_ref, coef,
    gat, send_own, recv_own, send_row, recv_row, basis, gram, ring_a, ring_b,
    tab_v, tab_s, lsem, tsem, ssem, rsem,
):
    row = lax.axis_index("by")
    me = lax.axis_index("bx")
    core = lax.rem(row, 2)
    below_row = lax.rem(row + 1, NBY)
    above_row = lax.rem(row + NBY - 1, NBY)
    step_a = 4 - 3 * core
    step_b = 1 + 3 * core
    px, py = me // 4, lax.rem(me, 4)
    a = px + core * (py - px)
    b = py + core * (px - py)

    def dev(i, j):
        return lax.rem(a + i, 4) * step_a + lax.rem(b + j, 4) * step_b

    barrier = pltpu.get_barrier_semaphore()

    def greet(**where):
        pl.semaphore_signal(barrier, inc=1, device_id=where, device_id_type=MESH)

    for i in range(1, NBX):
        greet(bx=lax.rem(me + i, NBX))
    for i in range(1, NBY):
        greet(by=lax.rem(row + i, NBY))
    for i in range(1, 4):
        greet(by=below_row, bx=dev(0, i))
        greet(by=above_row, bx=dev(0, i))
        greet(by=below_row, bx=dev(i, 0))
        greet(by=above_row, bx=dev(i, 0))
    greeted = NBX - 1 + NBY - 1 + 12

    local = [
        (cmap_hbm, cmap), (tmap_hbm, tmap), (buoy_hbm, buoy_ref), (wet_hbm, wet_ref), (prior_hbm, prior_ref), (land_hbm, land_ref),
        (speed_hbm, speed_ref), (diff_hbm, diff_ref), (patch_hbm, patch_ref),
    ]
    loads = [pltpu.make_async_copy(s, d, lsem.at[i]) for i, (s, d) in enumerate(local)]
    for load in loads:
        load.start()
    width = CELLS // CHUNKS
    streams = []
    for i in range(CHUNKS):
        part = (slice(None), slice(None), slice(None), pl.ds(i * width, width))
        streams.append(pltpu.make_async_copy(tr_hbm.at[part], tr.at[part], tsem.at[i]))
        streams[i].start()

    lane = lax.broadcasted_iota(jnp.int32, (1, BW), 1)
    sources = ((row, core, b), (above_row, 1 - core, a), (below_row, 1 - core, a))

    def fill(s, tabs):
        tabs = list(tabs)
        sx, sy, slot = s // 16, lax.rem(s // 4, 4), lax.rem(s, 4)
        for r, (which, its_core, its_b) in enumerate(sources):
            sa = sx + its_core * (sy - sx)
            sb = sy + its_core * (sx - sy)
            offset = lax.rem(its_b - sb + 4, 4)
            for kind, ref in enumerate((cmap, tmap)):
                hit = lane == lax.rem(ref[which * GBX + s], GBX)
                if r == 0:
                    tabs[kind] = jnp.where(hit, sa * BLOCKS + slot, tabs[kind])
                tabs[2 + 2 * r + kind] = jnp.where(hit, offset, tabs[2 + 2 * r + kind])
        return tuple(tabs)

    loads[0].wait()
    loads[1].wait()
    tabs = lax.fori_loop(0, GBX, fill, tuple(jnp.zeros((1, BW), jnp.int32) for _ in range(8)))
    for i in range(8):
        tab_v[pl.ds(i, 1), :] = tabs[i]
    load_tab = pltpu.make_async_copy(tab_v, tab_s, lsem.at[9])
    load_tab.start()

    mine = a * BLOCKS
    for load in loads[2:6]:
        load.wait()
    wet = wet_ref[...]
    total = jnp.zeros(wet.shape, jnp.float32)
    for k in range(LEV):
        total = total + jnp.where(wet > k, buoy_ref[k].astype(jnp.float32), 0.0)
    fields = (total, wet.astype(jnp.float32), prior_ref[...])
    for q in range(3):
        for n in range(BLOCKS):
            for r in range(BH):
                gat[mine + n, q, pl.ds(r, 1), :] = fields[q][n : n + 1, r * BW : (r + 1) * BW]
    for n in range(BLOCKS):
        gat[mine + n, 3] = land_ref[n].astype(jnp.float32)

    pl.semaphore_wait(barrier, greeted)

    def remote(src, dst, tag, where):
        copy = pltpu.make_async_remote_copy(
            src_ref=src, dst_ref=dst, send_sem=ssem.at[tag], recv_sem=rsem.at[tag],
            device_id=where, device_id_type=MESH,
        )
        copy.start()
        return copy

    chunk = gat.at[pl.ds(mine, BLOCKS)]
    first = [remote(chunk, chunk, i - 1, {"bx": dev(i, 0)}) for i in range(1, 4)]

    for load in loads[6:]:
        load.wait()

    def run_columns(part):
        per = width // 128
        for i in PARTS[part]:
            streams[i].wait()
        chunks = PARTS[part]

        def body(t, carry):
            columns(t, tr, speed_ref, diff_ref, wet_ref, patch_ref, coef)
            return carry

        lax.fori_loop(chunks.start * per, chunks.stop * per, body, 0)

    run_columns(0)
    load_tab.wait()
    for copy in first:
        copy.wait()

    lane8 = lax.broadcasted_iota(jnp.int32, (8, BW), 1)
    window_of = lane8 // 8

    def window(q, n, side):
        return (q % 2) * 8 + 2 * n + side

    def turned(v, shift):
        return pltpu.roll(v, shift % BW, 1) if shift % BW else v

    def pack(dst, role, i):
        its_row = (row, below_row, above_row)[role]
        base = its_row * GBX + dev(0, i) * BLOCKS
        place = {}
        for n in range(BLOCKS):
            g = lax.rem(tmap[base + n], GBX)
            for side, shift in ((0, 1), (1, GBX - 1), (2, 0)):
                at = lax.rem(g + shift, GBX)
                place[0, n, side] = tab_s[0, at]
                place[1, n, side] = tab_s[1, at]
        halves = ((0, 1), (1,), (0,))[role]
        names = range(3) if role == 0 else range(4)
        t = 0
        for n in range(BLOCKS):
            for q in names:
                for h in halves:
                    dst[t] = gat[place[q // 3, n, 2], q, pl.ds(8 * h, 8), :]
                    t += 1
        for pair in range(2):
            for h in halves:
                tile = jnp.zeros((8, BW), jnp.float32)
                for q in (2 * pair, 2 * pair + 1):
                    for n in range(BLOCKS):
                        for side in range(2):
                            w = window(q, n, side)
                            v = gat[place[q // 3, n, side], q, pl.ds(8 * h, 8), :]
                            v = turned(v, 8 * w + (8 if side else 0))
                            tile = jnp.where(window_of == w, v, tile)
                dst[t] = tile
                t += 1

    second = []
    for i in (2, 1, 3, 0):
        for d in range(2):
            buf = send_row.at[d, i]
            pack(buf, 1 + d, i)
            to = below_row if d == 0 else above_row
            second.append(
                remote(buf, recv_row.at[d, i], 6 + 4 * d + i, {"by": to, "bx": dev(0, i)})
            )
        if i:
            buf = send_own.at[i - 1]
            pack(buf, 0, i)
            second.append(remote(buf, recv_own.at[i], 2 + i, {"bx": dev(0, i)}))
        else:
            pack(recv_own.at[0], 0, 0)
    run_columns(1)
    for copy in second:
        copy.wait()

    has_north = (row > 0).astype(jnp.float32)
    has_south = (row < NBY - 1).astype(jnp.float32)
    acc = [None] * len(PAIRS)
    for n in range(BLOCKS):
        g = lax.rem(tmap[row * GBX + me * BLOCKS + n], GBX)
        around = [lax.rem(g + shift, GBX) for shift in (1, GBX - 1, 0)]
        came = {
            (src, kind, side): tab_s[2 + 2 * src + kind, around[side]]
            for src in range(3) for kind in range(2) for side in range(3)
        }

        def beside(buf, src, q, at):
            east = buf[came[src, q // 3, 0], at]
            west = buf[came[src, q // 3, 1], at]
            east = turned(east, BW - 8 * window(q, n, 0))
            west = turned(west, BW - 8 - 8 * window(q, n, 1))
            return jnp.where(lane8 < 8, east, jnp.where(lane8 >= BW - 8, west, 0.0))

        whole = []
        for q in range(4):
            kind = q // 3
            ends = []
            for d in range(2):
                buf = recv_row.at[d]
                middle = buf[came[1 + d, kind, 2], n * 4 + q]
                end = jnp.concatenate([middle, beside(buf, 1 + d, q, 16 + q // 2)], axis=1)
                if q == 3:
                    end = end * (has_north if d == 0 else has_south)
                ends.append(end)
            parts = [ends[0]]
            for h in range(2):
                if q < 3:
                    middle = recv_own[came[0, 0, 2], (n * 3 + q) * 2 + h]
                else:
                    middle = gat[mine + n, 3, pl.ds(8 * h, 8), :]
                side = beside(recv_own, 0, q, 24 + (q // 2) * 2 + h)
                parts.append(jnp.concatenate([middle, side], axis=1))
            parts.append(ends[1])
            whole.append(jnp.concatenate(parts, axis=0))
        force, depth, prior, ocean = whole
        rows = BH + 16

        def east(v):
            return pltpu.roll(v, LANES - 1, 1)

        def west(v):
            return pltpu.roll(v, 1, 1)

        def south_of(v):
            return pltpu.roll(v, rows - 1, 0)

        def north_of(v):
            return pltpu.roll(v, 1, 0)

        face_e = FACE * jnp.minimum(depth, east(depth)) * ocean * east(ocean)
        face_s = FACE * jnp.minimum(depth, south_of(depth)) * ocean * south_of(ocean)
        face_w, face_n = west(face_e), north_of(face_s)
        centre = SURFACE * ocean + (1.0 - ocean)
        diag = centre + face_e + face_w + face_s + face_n
        inv = 1.0 / diag
        centre, face_e, face_w = centre * inv, face_e * inv, face_w * inv
        face_s, face_n = face_s * inv, face_n * inv

        def scaled(v):
            out = centre * v + face_e * (v - east(v)) + face_w * (v - west(v))
            return out + face_s * (v - south_of(v)) + face_n * (v - north_of(v))

        def own(v):
            return v[8 : 8 + BH, :BW]

        guess = ocean * prior
        u = ocean * force * inv - scaled(guess)
        weight = own(diag)
        basis[n, ITERS] = own(guess)
        mine_of, weighted = [], []
        for k in range(ITERS + 1):
            mine_of.append(own(u))
            if k < ITERS:
                basis[n, k] = mine_of[k]
                weighted.append(weight * mine_of[k])
                image = scaled(u)
                u = image - SHIFTS[k] * u if SHIFTS[k] else image
        for e, (i, j) in enumerate(PAIRS):
            prod = weighted[i] * mine_of[j]
            prod = prod[:8] + prod[8:]
            acc[e] = prod if acc[e] is None else acc[e] + prod

    for e in range(len(PAIRS)):
        gram[pl.ds(e, 1), :] = jnp.sum(acc[e], axis=0, keepdims=True)
    gram[pl.ds(len(PAIRS), ENTRIES - len(PAIRS)), :] = jnp.zeros(
        (ENTRIES - len(PAIRS), BW), jnp.float32
    )
    on_diag = lax.broadcasted_iota(jnp.int32, (ENTRIES, BW), 0) == lax.broadcasted_iota(
        jnp.int32, (ENTRIES, BW), 1
    )
    placed = jnp.where(on_diag, jnp.sum(gram[...], axis=1, keepdims=True), 0.0)
    packed = placed[0:8] + placed[8:16] + placed[16:24] + placed[24:32]

    def all_sum(value, ring, index, count, axis, base, during):
        ring[index] = value
        sent = [
            remote(ring.at[index], ring.at[index], base + i, {axis: lax.rem(index + i, count)})
            for i in range(1, count)
        ]
        if during:
            run_columns(2)
        for copy in sent:
            copy.wait()
        return jnp.sum(ring[...], axis=0)

    packed = all_sum(packed, ring_a, me, NBX, "bx", 14, True)
    packed = all_sum(packed, ring_b, row, NBY, "by", 14 + NBX, False)
    line = jnp.sum(packed, axis=0, keepdims=True)
    spread = jnp.sum(jnp.where(on_diag, line, 0.0), axis=1, keepdims=True)
    spread = jnp.broadcast_to(spread, (ENTRIES, BW))
    g = {}
    for e, (i, j) in enumerate(PAIRS):
        g[i, j] = g[j, i] = spread[e : e + 1]

    def form(left, right):
        out = None
        for i, vi in enumerate(left):
            inner = None
            for j, vj in enumerate(right):
                term = g[i, j] * vj
                inner = term if inner is None else inner + term
            out = vi * inner if out is None else out + vi * inner
        return out

    one = jnp.ones((1, BW), jnp.float32)
    zero = jnp.zeros((1, BW), jnp.float32)
    p, z = [one], [one]
    x = [zero] * ITERS
    rz = g[0, 0]
    for it in range(ITERS):
        y = [SHIFTS[k] * p[k] if SHIFTS[k] else zero for k in range(it + 1)] + [zero]
        for k in range(it + 1):
            y[k + 1] = y[k + 1] + p[k]
        pq = form(p, y)
        live = jnp.logical_and(rz > 0.0, pq > 0.0)
        alpha = jnp.where(live, rz, 0.0) / jnp.where(live, pq, 1.0)
        alpha = jnp.minimum(alpha, ALPHA_MAX)
        for k in range(it + 1):
            x[k] = x[k] + alpha * p[k]
        if it + 1 < ITERS:
            z = [zk - alpha * yk for zk, yk in zip(z + [zero], y)]
            rz_new = jnp.maximum(form(z, z), 0.0)
            beta = jnp.where(live, rz_new, 0.0) / jnp.where(live, rz, 1.0)
            p = [zk + beta * pk for zk, pk in zip(z, p + [zero])]
            rz = rz_new
    for n in range(BLOCKS):
        height = basis[n, ITERS]
        for k in range(ITERS):
            height = height + x[k] * basis[n, k]
        out_ref[n] = height


def write_kernel(tr, height, tr_out, height_out, sem):
    width = CELLS // CHUNKS
    copies = [pltpu.make_async_copy(height, height_out, sem.at[CHUNKS])]
    for i in range(CHUNKS):
        part = (slice(None), slice(None), slice(None), pl.ds(i * width, width))
        copies.append(pltpu.make_async_copy(tr.at[part], tr_out.at[part], sem.at[i]))
    for copy in copies:
        copy.start()
    for copy in copies:
        copy.wait()


def local(
    tracers, vertical_speed, diffusivity, buoyancy_force, wet_levels, surface_patch,
    prior_height, land_mask, baroclinic_map, barotropic_map,
):
    f32, i32 = jnp.float32, jnp.int32
    vmem = pl.BlockSpec(memory_space=pltpu.VMEM)
    hbm = pl.BlockSpec(memory_space=pltpu.HBM)
    tags = 14 + NBX + NBY
    height_shape = (BLOCKS, BH, BW)
    tr, height = pl.pallas_call(
        step_kernel,
        out_shape=(pltpu.VMEM(tracers.shape, f32), pltpu.VMEM(height_shape, f32)),
        in_specs=[hbm] * 10,
        out_specs=(vmem, vmem),
        scratch_shapes=[
            pltpu.SMEM((NBY * GBX,), i32),
            pltpu.SMEM((NBY * GBX,), i32),
            pltpu.VMEM((LEV, BLOCKS, CELLS), jnp.bfloat16),
            pltpu.VMEM((BLOCKS, CELLS), i32),
            pltpu.VMEM((BLOCKS, CELLS), i32),
            pltpu.VMEM((BLOCKS, CELLS), f32),
            pltpu.VMEM(height_shape, i32),
            pltpu.VMEM((LEV, BLOCKS, CELLS), f32),
            pltpu.VMEM((LEV, BLOCKS, CELLS), f32),
            pltpu.VMEM((6, LEV, BLOCKS, 128), f32),
            pltpu.VMEM((4 * BLOCKS, 4, BH, BW), f32),
            pltpu.VMEM((3, OWN_TILES, 8, BW), f32),
            pltpu.VMEM((4, OWN_TILES, 8, BW), f32),
            pltpu.VMEM((2, 4, ROW_TILES, 8, BW), f32),
            pltpu.VMEM((2, 4, ROW_TILES, 8, BW), f32),
            pltpu.VMEM((BLOCKS, ITERS + 1, BH, BW), f32),
            pltpu.VMEM((ENTRIES, BW), f32),
            pltpu.VMEM((NBX, 8, BW), f32),
            pltpu.VMEM((NBY, 8, BW), f32),
            pltpu.VMEM((8, BW), i32),
            pltpu.SMEM((8, BW), i32),
            pltpu.SemaphoreType.DMA((10,)),
            pltpu.SemaphoreType.DMA((CHUNKS,)),
            pltpu.SemaphoreType.DMA((tags,)),
            pltpu.SemaphoreType.DMA((tags,)),
        ],
        compiler_params=pltpu.CompilerParams(
            collective_id=0, has_side_effects=True, vmem_limit_bytes=32 * 2**20
        ),
        name="step",
    )(
        *(
            pltpu.with_memory_space_constraint(array, pltpu.HBM)
            for array in (
                baroclinic_map, barotropic_map, buoyancy_force, wet_levels, surface_patch,
                prior_height, land_mask, vertical_speed, diffusivity, tracers,
            )
        )
    )
    return pl.pallas_call(
        write_kernel,
        out_shape=(
            jax.ShapeDtypeStruct(tracers.shape, f32), jax.ShapeDtypeStruct(height_shape, f32)
        ),
        in_specs=[vmem, vmem],
        out_specs=(hbm, hbm),
        scratch_shapes=[pltpu.SemaphoreType.DMA((CHUNKS + 1,))],
        compiler_params=pltpu.CompilerParams(vmem_limit_bytes=2 * 2**20),
        name="write",
    )(tr, height)


def solution(mesh):
    return jax.shard_map(
        local,
        mesh=mesh,
        in_specs=(
            P(None, ("by", "bx"), None, None),
            P(None, ("by", "bx"), None),
            P(None, ("by", "bx"), None),
            P(None, ("by", "bx"), None),
            P(("by", "bx"), None),
            P(("by", "bx"), None),
            P(("by", "bx"), None),
            P(("by", "bx"), None, None),
            P(),
            P(),
        ),
        out_specs=(P(None, ("by", "bx"), None, None), P(("by", "bx"), None, None)),
        check_vma=False,
    )
```

time: 65.6 us -> 39.4 us (0.60)
  Pallas kernels: 53.3 us -> 38.7 us
  between operations: 6.46 us -> 0.64 us
  local copies, waits for them, and re-layouts: 2.79 us -> 0 us
  other arithmetic: 2.67 us -> 0 us
    pallas_call x2, Pallas kernels: 53.3 us -> 38.7 us  [the longest x1 34.6 us: local(): pl.pallas_call(step_kernel, out_shape=(pltpu.VMEM(tracers.shape, f32), pl...]
    select_n x3 -> x0, other arithmetic: 1.42 us -> none  [the longest x1 0.74 us: index_table(): wanted = (wanted[:, :, None] + sides + GBX) % GBX]
    reshape x2 -> x0, local copies, waits for them, and re-layouts: 1.41 us -> none  [the longest x1 0.79 us: index_table(): blocks = barotropic_map.reshape(NBY, NBX, BLOCKS)]
    another operation x2 -> x0, other arithmetic: 0.78 us -> none  [index_table(): held = jnp.stack([clinic, tropic])]
where the time goes in v2:
time: 39.4 us; the launch traced here: 39.3 us
  Pallas kernels  38.7 us (98%)
  between operations  0.64 us (2%)
    pallas_call x1, Pallas kernels, local(): pl.pallas_call(step_kernel, out_shape=(pltpu.VMEM(tracers.shape, f32), pl...  34.6 us
    pallas_call x1, Pallas kernels, local(): pl.pallas_call(write_kernel, out_shape=(jax.ShapeDtypeStruct(tracers.shap...  4.05 us

profile of v2, /device:TPU:1, one launch (start us, length us, event | category | flops | bytes accessed | tf_op | source)
XLA Modules:
  0.0 39.3 jit_solution(114881548906907222)
XLA Ops:
  0.6 34.6 %step.1 = (f32[20,4,16,2048]{3,2,1,0:T(8,128)S(1)}, f32[4,16,128]{2,1,0:T(8,128)S(1)}) custom-call(s32[512]{0:T(512)} %cmap_hbm.1, s32[512]{0:T(512)} %tmap_hbm.1, bf16[20,4,2048]{2,1,0:T(4,128)(2,1)} %buoy_hbm.1, s32[4,2048]{1,0:T(4,128)} %wet_hbm.1, s32[4,2048]{1,0:T(4,128)} %patch_hbm.1, f32[4,2048]{1,0:T(4,128)} %prior_hbm.1, s32[4,16,128]{2,1,0:T(8,128)} %land_hbm.1, ...), custom_call_target="tpu_custom_call" | custom-call | tf_op jit(solution)/shard_map/step/pallas_call | solution.py:443
  35.3 4.1 %write.1 = (f32[20,4,16,2048]{3,2,1,0:T(8,128)}, f32[4,16,128]{2,1,0:T(8,128)}) custom-call(f32[20,4,16,2048]{3,2,1,0:T(8,128)S(1)} %get-tuple-element.4.tr, f32[4,16,128]{2,1,0:T(8,128)S(1)} %get-tuple-element.5.height), custom_call_target="tpu_custom_call" | custom-call | tf_op jit(solution)/shard_map/write/pallas_call | solution.py:488

commit v3 on v2

--- a/solution.py
+++ b/solution.py
@@ -20,9 +20,11 @@
 PAIRS = [(i, j) for i in range(ITERS) for j in range(i, ITERS + 1)]
 ENTRIES = 32
 CHUNKS = 8
-PARTS = (range(0, 2), range(2, 5), range(5, 8))
-OWN_TILES = BLOCKS * 3 * 2 + 4
-ROW_TILES = BLOCKS * 4 + 2
+PARTS = (range(0, 1), range(1, 5), range(5, 8))
+OWN_PART = ((0, 18), (18, 10))
+ROW_PART = ((0, 9), (9, 9))
+DEVICES = NBX * NBY
+SUM_TAG = 28
 
 
 def columns(tile, tr, speed_ref, diff_ref, wet_ref, patch_ref, coef):
@@ -83,8 +85,8 @@
     cmap_hbm, tmap_hbm, buoy_hbm, wet_hbm, patch_hbm, prior_hbm, land_hbm, speed_hbm, diff_hbm, tr_hbm,
     tr, out_ref,
     cmap, tmap, buoy_ref, wet_ref, patch_ref, prior_ref, land_ref, speed_ref, diff_ref, coef,
-    gat, send_own, recv_own, send_row, recv_row, basis, gram, ring_a, ring_b,
-    tab_v, tab_s, lsem, tsem, ssem, rsem,
+    depths, forces, send_own, recv_own, send_row, recv_row, basis, gram, ring,
+    tab_v, tab_s, plane_sem, all_sem, lsem, tsem, ssem, rsem,
 ):
     row = lax.axis_index("by")
     me = lax.axis_index("bx")
@@ -105,23 +107,67 @@
     def greet(**where):
         pl.semaphore_signal(barrier, inc=1, device_id=where, device_id_type=MESH)
 
-    for i in range(1, NBX):
-        greet(bx=lax.rem(me + i, NBX))
-    for i in range(1, NBY):
-        greet(by=lax.rem(row + i, NBY))
     for i in range(1, 4):
+        greet(bx=dev(i, 0))
+        greet(bx=dev(0, i))
         greet(by=below_row, bx=dev(0, i))
         greet(by=above_row, bx=dev(0, i))
         greet(by=below_row, bx=dev(i, 0))
         greet(by=above_row, bx=dev(i, 0))
-    greeted = NBX - 1 + NBY - 1 + 12
+    for i in range(1, NBY):
+        greet(by=lax.rem(row + i, NBY))
+    greeted = 6 * 3 + NBY - 1
 
     local = [
-        (cmap_hbm, cmap), (tmap_hbm, tmap), (buoy_hbm, buoy_ref), (wet_hbm, wet_ref), (prior_hbm, prior_ref), (land_hbm, land_ref),
+        (wet_hbm, wet_ref), (prior_hbm, prior_ref), (buoy_hbm, buoy_ref), (land_hbm, land_ref),
+        (cmap_hbm, cmap), (tmap_hbm, tmap),
         (speed_hbm, speed_ref), (diff_hbm, diff_ref), (patch_hbm, patch_ref),
     ]
     loads = [pltpu.make_async_copy(s, d, lsem.at[i]) for i, (s, d) in enumerate(local)]
-    for load in loads:
+    for load in loads[:6]:
+        load.start()
+
+    def remote(src, dst, tag, where):
+        copy = pltpu.make_async_remote_copy(
+            src_ref=src, dst_ref=dst, send_sem=ssem.at[tag], recv_sem=rsem.at[tag],
+            device_id=where, device_id_type=MESH,
+        )
+        copy.start()
+        return copy
+
+    mine = a * BLOCKS
+    gat = (depths, forces)
+
+    def place_field(pair, q, value):
+        for n in range(BLOCKS):
+            for r in range(BH):
+                gat[pair][mine + n, q, pl.ds(r, 1), :] = value[n : n + 1, r * BW : (r + 1) * BW]
+
+    def share(pair):
+        chunk = gat[pair].at[pl.ds(mine, BLOCKS)]
+        return [remote(chunk, chunk, 3 * pair + i - 1, {"bx": dev(i, 0)}) for i in range(1, 4)]
+
+    loads[0].wait()
+    loads[1].wait()
+    wet = wet_ref[...]
+    place_field(0, 0, wet.astype(jnp.float32))
+    place_field(0, 1, prior_ref[...])
+    pl.semaphore_wait(barrier, greeted)
+    first = [share(0)]
+    for i in range(1, 4):
+        pl.semaphore_signal(plane_sem, inc=1, device_id={"bx": dev(0, i)}, device_id_type=MESH)
+
+    loads[2].wait()
+    loads[3].wait()
+    total = jnp.zeros(wet.shape, jnp.float32)
+    for k in range(LEV):
+        total = total + jnp.where(wet > k, buoy_ref[k].astype(jnp.float32), 0.0)
+    place_field(1, 0, total)
+    for n in range(BLOCKS):
+        gat[1][mine + n, 1] = land_ref[n].astype(jnp.float32)
+    first.append(share(1))
+
+    for load in loads[6:]:
         load.start()
     width = CELLS // CHUNKS
     streams = []
@@ -147,42 +193,19 @@
                 tabs[2 + 2 * r + kind] = jnp.where(hit, offset, tabs[2 + 2 * r + kind])
         return tuple(tabs)
 
-    loads[0].wait()
-    loads[1].wait()
+    loads[4].wait()
+    loads[5].wait()
     tabs = lax.fori_loop(0, GBX, fill, tuple(jnp.zeros((1, BW), jnp.int32) for _ in range(8)))
     for i in range(8):
         tab_v[pl.ds(i, 1), :] = tabs[i]
     load_tab = pltpu.make_async_copy(tab_v, tab_s, lsem.at[9])
     load_tab.start()
 
-    mine = a * BLOCKS
-    for load in loads[2:6]:
-        load.wait()
-    wet = wet_ref[...]
-    total = jnp.zeros(wet.shape, jnp.float32)
-    for k in range(LEV):
-        total = total + jnp.where(wet > k, buoy_ref[k].astype(jnp.float32), 0.0)
-    fields = (total, wet.astype(jnp.float32), prior_ref[...])
-    for q in range(3):
-        for n in range(BLOCKS):
-            for r in range(BH):
-                gat[mine + n, q, pl.ds(r, 1), :] = fields[q][n : n + 1, r * BW : (r + 1) * BW]
-    for n in range(BLOCKS):
-        gat[mine + n, 3] = land_ref[n].astype(jnp.float32)
-
-    pl.semaphore_wait(barrier, greeted)
-
-    def remote(src, dst, tag, where):
-        copy = pltpu.make_async_remote_copy(
-            src_ref=src, dst_ref=dst, send_sem=ssem.at[tag], recv_sem=rsem.at[tag],
-            device_id=where, device_id_type=MESH,
+    pl.semaphore_wait(plane_sem, 3)
+    for i in range(1, NBY):
+        pl.semaphore_signal(
+            all_sem, inc=1, device_id={"by": lax.rem(row + i, NBY)}, device_id_type=MESH
         )
-        copy.start()
-        return copy
-
-    chunk = gat.at[pl.ds(mine, BLOCKS)]
-    first = [remote(chunk, chunk, i - 1, {"bx": dev(i, 0)}) for i in range(1, 4)]
-
     for load in loads[6:]:
         load.wait()
 
@@ -198,21 +221,21 @@
 
         lax.fori_loop(chunks.start * per, chunks.stop * per, body, 0)
 
-    run_columns(0)
     load_tab.wait()
-    for copy in first:
-        copy.wait()
 
     lane8 = lax.broadcasted_iota(jnp.int32, (8, BW), 1)
     window_of = lane8 // 8
 
     def window(q, n, side):
-        return (q % 2) * 8 + 2 * n + side
+        return q * 8 + 2 * n + side
+
+    def kind_of(pair, q):
+        return 1 if (pair, q) == (1, 1) else 0
 
     def turned(v, shift):
         return pltpu.roll(v, shift % BW, 1) if shift % BW else v
 
-    def pack(dst, role, i):
+    def pack(dst, pair, role, i):
         its_row = (row, below_row, above_row)[role]
         base = its_row * GBX + dev(0, i) * BLOCKS
         place = {}
@@ -220,44 +243,54 @@
             g = lax.rem(tmap[base + n], GBX)
             for side, shift in ((0, 1), (1, GBX - 1), (2, 0)):
                 at = lax.rem(g + shift, GBX)
-                place[0, n, side] = tab_s[0, at]
-                place[1, n, side] = tab_s[1, at]
+                for kind in range(1 + pair):
+                    place[kind, n, side] = tab_s[kind, at]
         halves = ((0, 1), (1,), (0,))[role]
-        names = range(3) if role == 0 else range(4)
-        t = 0
+        t = (OWN_PART if role == 0 else ROW_PART)[pair][0]
         for n in range(BLOCKS):
-            for q in names:
+            for q in range(1 if (role, pair) == (0, 1) else 2):
                 for h in halves:
-                    dst[t] = gat[place[q // 3, n, 2], q, pl.ds(8 * h, 8), :]
+                    dst[t] = gat[pair][place[kind_of(pair, q), n, 2], q, pl.ds(8 * h, 8), :]
                     t += 1
-        for pair in range(2):
-            for h in halves:
-                tile = jnp.zeros((8, BW), jnp.float32)
-                for q in (2 * pair, 2 * pair + 1):
-                    for n in range(BLOCKS):
-                        for side in range(2):
-                            w = window(q, n, side)
-                            v = gat[place[q // 3, n, side], q, pl.ds(8 * h, 8), :]
-                            v = turned(v, 8 * w + (8 if side else 0))
-                            tile = jnp.where(window_of == w, v, tile)
-                dst[t] = tile
-                t += 1
+        for h in halves:
+            tile = jnp.zeros((8, BW), jnp.float32)
+            for q in range(2):
+                for n in range(BLOCKS):
+                    for side in range(2):
+                        w = window(q, n, side)
+                        v = gat[pair][place[kind_of(pair, q), n, side], q, pl.ds(8 * h, 8), :]
+                        v = turned(v, 8 * w + (8 if side else 0))
+                        tile = jnp.where(window_of == w, v, tile)
+            dst[t] = tile
+            t += 1
 
     second = []
-    for i in (2, 1, 3, 0):
-        for d in range(2):
-            buf = send_row.at[d, i]
-            pack(buf, 1 + d, i)
-            to = below_row if d == 0 else above_row
-            second.append(
-                remote(buf, recv_row.at[d, i], 6 + 4 * d + i, {"by": to, "bx": dev(0, i)})
-            )
-        if i:
-            buf = send_own.at[i - 1]
-            pack(buf, 0, i)
-            second.append(remote(buf, recv_own.at[i], 2 + i, {"bx": dev(0, i)}))
-        else:
-            pack(recv_own.at[0], 0, 0)
+    for pair in range(2):
+        for copy in first[pair]:
+            copy.wait()
+        row_part, own_part = pl.ds(*ROW_PART[pair]), pl.ds(*OWN_PART[pair])
+        for i in (2, 1, 3, 0):
+            for d in range(2):
+                pack(send_row.at[d, i], pair, 1 + d, i)
+                to = below_row if d == 0 else above_row
+                second.append(
+                    remote(
+                        send_row.at[d, i, row_part], recv_row.at[d, i, row_part],
+                        12 + 8 * pair + 4 * d + i, {"by": to, "bx": dev(0, i)},
+                    )
+                )
+            if i:
+                pack(send_own.at[i - 1], pair, 0, i)
+                second.append(
+                    remote(
+                        send_own.at[i - 1, own_part], recv_own.at[i, own_part],
+                        5 + 3 * pair + i, {"bx": dev(0, i)},
+                    )
+                )
+            else:
+                pack(recv_own.at[0], pair, 0, 0)
+        if pair == 0:
+            run_columns(0)
     run_columns(1)
     for copy in second:
         copy.wait()
@@ -273,35 +306,40 @@
             for src in range(3) for kind in range(2) for side in range(3)
         }
 
-        def beside(buf, src, q, at):
-            east = buf[came[src, q // 3, 0], at]
-            west = buf[came[src, q // 3, 1], at]
-            east = turned(east, BW - 8 * window(q, n, 0))
-            west = turned(west, BW - 8 - 8 * window(q, n, 1))
+        def beside(buf, src, pair, q, at):
+            kind = kind_of(pair, q)
+            east = turned(buf[came[src, kind, 0], at], BW - 8 * window(q, n, 0))
+            west = turned(buf[came[src, kind, 1], at], BW - 8 - 8 * window(q, n, 1))
             return jnp.where(lane8 < 8, east, jnp.where(lane8 >= BW - 8, west, 0.0))
 
-        whole = []
-        for q in range(4):
-            kind = q // 3
-            ends = []
-            for d in range(2):
-                buf = recv_row.at[d]
-                middle = buf[came[1 + d, kind, 2], n * 4 + q]
-                end = jnp.concatenate([middle, beside(buf, 1 + d, q, 16 + q // 2)], axis=1)
-                if q == 3:
-                    end = end * (has_north if d == 0 else has_south)
-                ends.append(end)
-            parts = [ends[0]]
-            for h in range(2):
-                if q < 3:
-                    middle = recv_own[came[0, 0, 2], (n * 3 + q) * 2 + h]
-                else:
-                    middle = gat[mine + n, 3, pl.ds(8 * h, 8), :]
-                side = beside(recv_own, 0, q, 24 + (q // 2) * 2 + h)
-                parts.append(jnp.concatenate([middle, side], axis=1))
-            parts.append(ends[1])
-            whole.append(jnp.concatenate(parts, axis=0))
-        force, depth, prior, ocean = whole
+        whole = {}
+        for pair in range(2):
+            row_base, own_base = ROW_PART[pair][0], OWN_PART[pair][0]
+            for q in range(2):
+                kind = kind_of(pair, q)
+                ends = []
+                for d in range(2):
+                    buf = recv_row.at[d]
+                    middle = buf[came[1 + d, kind, 2], row_base + n * 2 + q]
+                    side = beside(buf, 1 + d, pair, q, row_base + 8)
+                    end = jnp.concatenate([middle, side], axis=1)
+                    if kind:
+                        end = end * (has_north if d == 0 else has_south)
+                    ends.append(end)
+                parts = [ends[0]]
+                for h in range(2):
+                    if kind:
+                        middle = gat[1][mine + n, 1, pl.ds(8 * h, 8), :]
+                    elif pair:
+                        middle = recv_own[came[0, 0, 2], own_base + n * 2 + h]
+                    else:
+                        middle = recv_own[came[0, 0, 2], own_base + (n * 2 + q) * 2 + h]
+                    edges = own_base + (8 if pair else 16)
+                    side = beside(recv_own, 0, pair, q, edges + h)
+                    parts.append(jnp.concatenate([middle, side], axis=1))
+                parts.append(ends[1])
+                whole[pair, q] = jnp.concatenate(parts, axis=0)
+        depth, prior, force, ocean = whole[0, 0], whole[0, 1], whole[1, 0], whole[1, 1]
         rows = BH + 16
 
         def east(v):
@@ -360,21 +398,17 @@
     placed = jnp.where(on_diag, jnp.sum(gram[...], axis=1, keepdims=True), 0.0)
     packed = placed[0:8] + placed[8:16] + placed[16:24] + placed[24:32]
 
-    def all_sum(value, ring, index, count, axis, base, during):
-        ring[index] = value
-        sent = [
-            remote(ring.at[index], ring.at[index], base + i, {axis: lax.rem(index + i, count)})
-            for i in range(1, count)
-        ]
-        if during:
-            run_columns(2)
-        for copy in sent:
-            copy.wait()
-        return jnp.sum(ring[...], axis=0)
-
-    packed = all_sum(packed, ring_a, me, NBX, "bx", 14, True)
-    packed = all_sum(packed, ring_b, row, NBY, "by", 14 + NBX, False)
-    line = jnp.sum(packed, axis=0, keepdims=True)
+    pl.semaphore_wait(all_sem, NBY - 1)
+    flat = row * NBX + me
+    ring[flat] = jnp.sum(packed, axis=0, keepdims=True)
+    for i in range(1, DEVICES):
+        to = lax.rem(flat + i, DEVICES)
+        remote(ring.at[flat], ring.at[flat], SUM_TAG, {"by": to // NBX, "bx": lax.rem(to, NBX)})
+    run_columns(2)
+    others = ring.at[pl.ds(0, DEVICES - 1)]
+    pltpu.make_async_copy(others, others, rsem.at[SUM_TAG]).wait()
+    pltpu.make_async_copy(others, others, ssem.at[SUM_TAG]).wait()
+    line = jnp.sum(ring[...], axis=0)
     spread = jnp.sum(jnp.where(on_diag, line, 0.0), axis=1, keepdims=True)
     spread = jnp.broadcast_to(spread, (ENTRIES, BW))
     g = {}
@@ -438,7 +472,7 @@
     f32, i32 = jnp.float32, jnp.int32
     vmem = pl.BlockSpec(memory_space=pltpu.VMEM)
     hbm = pl.BlockSpec(memory_space=pltpu.HBM)
-    tags = 14 + NBX + NBY
+    tags = SUM_TAG + 1
     height_shape = (BLOCKS, BH, BW)
     tr, height = pl.pallas_call(
         step_kernel,
@@ -456,17 +490,19 @@
             pltpu.VMEM((LEV, BLOCKS, CELLS), f32),
             pltpu.VMEM((LEV, BLOCKS, CELLS), f32),
             pltpu.VMEM((6, LEV, BLOCKS, 128), f32),
-            pltpu.VMEM((4 * BLOCKS, 4, BH, BW), f32),
-            pltpu.VMEM((3, OWN_TILES, 8, BW), f32),
-            pltpu.VMEM((4, OWN_TILES, 8, BW), f32),
-            pltpu.VMEM((2, 4, ROW_TILES, 8, BW), f32),
-            pltpu.VMEM((2, 4, ROW_TILES, 8, BW), f32),
+            pltpu.VMEM((4 * BLOCKS, 2, BH, BW), f32),
+            pltpu.VMEM((4 * BLOCKS, 2, BH, BW), f32),
+            pltpu.VMEM((3, 28, 8, BW), f32),
+            pltpu.VMEM((4, 28, 8, BW), f32),
+            pltpu.VMEM((2, 4, 18, 8, BW), f32),
+            pltpu.VMEM((2, 4, 18, 8, BW), f32),
             pltpu.VMEM((BLOCKS, ITERS + 1, BH, BW), f32),
             pltpu.VMEM((ENTRIES, BW), f32),
-            pltpu.VMEM((NBX, 8, BW), f32),
-            pltpu.VMEM((NBY, 8, BW), f32),
+            pltpu.VMEM((DEVICES, 1, BW), f32),
             pltpu.VMEM((8, BW), i32),
             pltpu.SMEM((8, BW), i32),
+            pltpu.SemaphoreType.REGULAR,
+            pltpu.SemaphoreType.REGULAR,
             pltpu.SemaphoreType.DMA((10,)),
             pltpu.SemaphoreType.DMA((CHUNKS,)),
             pltpu.SemaphoreType.DMA((tags,)),

time: 39.4 us -> 34.6 us (0.88)
  Pallas kernels: 38.7 us -> 33.8 us
    pallas_call x1, Pallas kernels: 34.6 us -> 29.8 us  [local(): pl.pallas_call(step_kernel, out_shape=(pltpu.VMEM(tracers.shape, f32), pl...]
where the time goes in v3:
time: 34.6 us; the launch traced here: 34.5 us
  Pallas kernels  33.8 us (98%)
  between operations  0.64 us (2%)
    pallas_call x1, Pallas kernels, local(): pl.pallas_call(step_kernel, out_shape=(pltpu.VMEM(tracers.shape, f32), pl...  29.8 us
    pallas_call x1, Pallas kernels, local(): pl.pallas_call(write_kernel, out_shape=(jax.ShapeDtypeStruct(tracers.shap...  4.05 us

profile of v3, /device:TPU:1, one launch (start us, length us, event | category | flops | bytes accessed | tf_op | source)
XLA Modules:
  0.0 34.5 jit_solution(8483727032565606161)
XLA Ops:
  0.6 29.8 %step.1 = (f32[20,4,16,2048]{3,2,1,0:T(8,128)S(1)}, f32[4,16,128]{2,1,0:T(8,128)S(1)}) custom-call(s32[512]{0:T(512)} %cmap_hbm.1, s32[512]{0:T(512)} %tmap_hbm.1, bf16[20,4,2048]{2,1,0:T(4,128)(2,1)} %buoy_hbm.1, s32[4,2048]{1,0:T(4,128)} %wet_hbm.1, s32[4,2048]{1,0:T(4,128)} %patch_hbm.1, f32[4,2048]{1,0:T(4,128)} %prior_hbm.1, s32[4,16,128]{2,1,0:T(8,128)} %land_hbm.1, ...), custom_call_target="tpu_custom_call" | custom-call | tf_op jit(solution)/shard_map/step/pallas_call | solution.py:477
  30.4 4.1 %write.1 = (f32[20,4,16,2048]{3,2,1,0:T(8,128)}, f32[4,16,128]{2,1,0:T(8,128)}) custom-call(f32[20,4,16,2048]{3,2,1,0:T(8,128)S(1)} %get-tuple-element.4.tr, f32[4,16,128]{2,1,0:T(8,128)S(1)} %get-tuple-element.5.height), custom_call_target="tpu_custom_call" | custom-call | tf_op jit(solution)/shard_map/write/pallas_call | solution.py:524

commit v4 on v3

--- a/solution.py
+++ b/solution.py
@@ -25,6 +25,10 @@
 ROW_PART = ((0, 9), (9, 9))
 DEVICES = NBX * NBY
 SUM_TAG = 28
+FAR_FIRST = sorted(
+    [(z, c, x, y) for z in range(4) for c in range(2) for x in range(4) for y in range(4)][1:],
+    key=lambda o: -sum(min(k, 4 - k) for k in (o[0], o[2], o[3])),
+)
 
 
 def columns(tile, tr, speed_ref, diff_ref, wet_ref, patch_ref, coef):
@@ -86,7 +90,7 @@
     tr, out_ref,
     cmap, tmap, buoy_ref, wet_ref, patch_ref, prior_ref, land_ref, speed_ref, diff_ref, coef,
     depths, forces, send_own, recv_own, send_row, recv_row, basis, gram, ring,
-    tab_v, tab_s, plane_sem, all_sem, lsem, tsem, ssem, rsem,
+    tab_v, tab_s, halo_sem, plane_sem, all_sem, lsem, tsem, ssem, rsem,
 ):
     row = lax.axis_index("by")
     me = lax.axis_index("bx")
@@ -110,13 +114,9 @@
     for i in range(1, 4):
         greet(bx=dev(i, 0))
         greet(bx=dev(0, i))
-        greet(by=below_row, bx=dev(0, i))
-        greet(by=above_row, bx=dev(0, i))
-        greet(by=below_row, bx=dev(i, 0))
-        greet(by=above_row, bx=dev(i, 0))
     for i in range(1, NBY):
         greet(by=lax.rem(row + i, NBY))
-    greeted = 6 * 3 + NBY - 1
+    greeted = 2 * 3 + NBY - 1
 
     local = [
         (wet_hbm, wet_ref), (prior_hbm, prior_ref), (buoy_hbm, buoy_ref), (land_hbm, land_ref),
@@ -145,7 +145,7 @@
 
     def share(pair):
         chunk = gat[pair].at[pl.ds(mine, BLOCKS)]
-        return [remote(chunk, chunk, 3 * pair + i - 1, {"bx": dev(i, 0)}) for i in range(1, 4)]
+        return [remote(chunk, chunk, 3 * pair + i - 1, {"bx": dev(i, 0)}) for i in (2, 1, 3)]
 
     loads[0].wait()
     loads[1].wait()
@@ -154,6 +154,8 @@
     place_field(0, 1, prior_ref[...])
     pl.semaphore_wait(barrier, greeted)
     first = [share(0)]
+    for to in (below_row, above_row):
+        pl.semaphore_signal(halo_sem, inc=1, device_id={"by": to}, device_id_type=MESH)
     for i in range(1, 4):
         pl.semaphore_signal(plane_sem, inc=1, device_id={"bx": dev(0, i)}, device_id_type=MESH)
 
@@ -206,10 +208,10 @@
         pl.semaphore_signal(
             all_sem, inc=1, device_id={"by": lax.rem(row + i, NBY)}, device_id_type=MESH
         )
-    for load in loads[6:]:
-        load.wait()
-
     def run_columns(part):
+        if part == 0:
+            for load in loads[6:]:
+                load.wait()
         per = width // 128
         for i in PARTS[part]:
             streams[i].wait()
@@ -264,10 +266,11 @@
             dst[t] = tile
             t += 1
 
+    pl.semaphore_wait(halo_sem, 2)
     second = []
     for pair in range(2):
         for copy in first[pair]:
-            copy.wait()
+            copy.wait_recv()
         row_part, own_part = pl.ds(*ROW_PART[pair]), pl.ds(*OWN_PART[pair])
         for i in (2, 1, 3, 0):
             for d in range(2):
@@ -293,7 +296,7 @@
             run_columns(0)
     run_columns(1)
     for copy in second:
-        copy.wait()
+        copy.wait_recv()
 
     has_north = (row > 0).astype(jnp.float32)
     has_south = (row < NBY - 1).astype(jnp.float32)
@@ -401,13 +404,13 @@
     pl.semaphore_wait(all_sem, NBY - 1)
     flat = row * NBX + me
     ring[flat] = jnp.sum(packed, axis=0, keepdims=True)
-    for i in range(1, DEVICES):
-        to = lax.rem(flat + i, DEVICES)
-        remote(ring.at[flat], ring.at[flat], SUM_TAG, {"by": to // NBX, "bx": lax.rem(to, NBX)})
+    for dz, dc, dx, dy in FAR_FIRST:
+        to_row = lax.rem(row // 2 + dz, 4) * 2 + lax.rem(core + dc, 2)
+        to = lax.rem(px + dx, 4) * 4 + lax.rem(py + dy, 4)
+        remote(ring.at[flat], ring.at[flat], SUM_TAG, {"by": to_row, "bx": to})
     run_columns(2)
     others = ring.at[pl.ds(0, DEVICES - 1)]
     pltpu.make_async_copy(others, others, rsem.at[SUM_TAG]).wait()
-    pltpu.make_async_copy(others, others, ssem.at[SUM_TAG]).wait()
     line = jnp.sum(ring[...], axis=0)
     spread = jnp.sum(jnp.where(on_diag, line, 0.0), axis=1, keepdims=True)
     spread = jnp.broadcast_to(spread, (ENTRIES, BW))
@@ -446,6 +449,9 @@
             beta = jnp.where(live, rz_new, 0.0) / jnp.where(live, rz, 1.0)
             p = [zk + beta * pk for zk, pk in zip(z, p + [zero])]
             rz = rz_new
+    pltpu.make_async_copy(others, others, ssem.at[SUM_TAG]).wait()
+    for copy in first[0] + first[1] + second:
+        copy.wait_send()
     for n in range(BLOCKS):
         height = basis[n, ITERS]
         for k in range(ITERS):
@@ -503,6 +509,7 @@
             pltpu.SMEM((8, BW), i32),
             pltpu.SemaphoreType.REGULAR,
             pltpu.SemaphoreType.REGULAR,
+            pltpu.SemaphoreType.REGULAR,
             pltpu.SemaphoreType.DMA((10,)),
             pltpu.SemaphoreType.DMA((CHUNKS,)),
             pltpu.SemaphoreType.DMA((tags,)),

time: 34.6 us -> 33.8 us (0.977)
  Pallas kernels: 33.8 us -> 33 us
    pallas_call x1, Pallas kernels: 29.8 us -> 29 us  [local(): pl.pallas_call(step_kernel, out_shape=(pltpu.VMEM(tracers.shape, f32), pl...]
where the time goes in v4:
time: 33.8 us; the launch traced here: 33.7 us
  Pallas kernels  33 us (98%)
  between operations  0.64 us (2%)
    pallas_call x1, Pallas kernels, local(): pl.pallas_call(step_kernel, out_shape=(pltpu.VMEM(tracers.shape, f32), pl...  29 us
    pallas_call x1, Pallas kernels, local(): pl.pallas_call(write_kernel, out_shape=(jax.ShapeDtypeStruct(tracers.shap...  4.05 us

profile of v4, /device:TPU:1, one launch (start us, length us, event | category | flops | bytes accessed | tf_op | source)
XLA Modules:
  0.0 33.7 jit_solution(13184354137865064320)
XLA Ops:
  0.6 29.0 %step.1 = (f32[20,4,16,2048]{3,2,1,0:T(8,128)S(1)}, f32[4,16,128]{2,1,0:T(8,128)S(1)}) custom-call(s32[512]{0:T(512)} %cmap_hbm.1, s32[512]{0:T(512)} %tmap_hbm.1, bf16[20,4,2048]{2,1,0:T(4,128)(2,1)} %buoy_hbm.1, s32[4,2048]{1,0:T(4,128)} %wet_hbm.1, s32[4,2048]{1,0:T(4,128)} %patch_hbm.1, f32[4,2048]{1,0:T(4,128)} %prior_hbm.1, s32[4,16,128]{2,1,0:T(8,128)} %land_hbm.1, ...), custom_call_target="tpu_custom_call" | custom-call | tf_op jit(solution)/shard_map/step/pallas_call | solution.py:483
  29.6 4.1 %write.1 = (f32[20,4,16,2048]{3,2,1,0:T(8,128)}, f32[4,16,128]{2,1,0:T(8,128)}) custom-call(f32[20,4,16,2048]{3,2,1,0:T(8,128)S(1)} %get-tuple-element.4.tr, f32[4,16,128]{2,1,0:T(8,128)S(1)} %get-tuple-element.5.height), custom_call_target="tpu_custom_call" | custom-call | tf_op jit(solution)/shard_map/write/pallas_call | solution.py:531

commit v5 on v4

--- a/solution.py
+++ b/solution.py
@@ -83,6 +83,13 @@
         for k in range(LEV - 2, -1, -1):
             follow = values[k] + c(4, k) * follow
             tr[k, n, :, sl] = follow
+
+
+def tree_sum(terms):
+    while len(terms) > 1:
+        pairs = [terms[k] + terms[k + 1] for k in range(0, len(terms) - 1, 2)]
+        terms = pairs + terms[len(pairs) * 2 :]
+    return terms[0]
 
 
 def step_kernel(
@@ -411,7 +418,7 @@
     run_columns(2)
     others = ring.at[pl.ds(0, DEVICES - 1)]
     pltpu.make_async_copy(others, others, rsem.at[SUM_TAG]).wait()
-    line = jnp.sum(ring[...], axis=0)
+    line = tree_sum([ring[k] for k in range(DEVICES)])
     spread = jnp.sum(jnp.where(on_diag, line, 0.0), axis=1, keepdims=True)
     spread = jnp.broadcast_to(spread, (ENTRIES, BW))
     g = {}
@@ -419,14 +426,8 @@
         g[i, j] = g[j, i] = spread[e : e + 1]
 
     def form(left, right):
-        out = None
-        for i, vi in enumerate(left):
-            inner = None
-            for j, vj in enumerate(right):
-                term = g[i, j] * vj
-                inner = term if inner is None else inner + term
-            out = vi * inner if out is None else out + vi * inner
-        return out
+        inner = [tree_sum([g[i, j] * vj for j, vj in enumerate(right)]) for i in range(len(left))]
+        return tree_sum([vi * w for vi, w in zip(left, inner)])
 
     one = jnp.ones((1, BW), jnp.float32)
     zero = jnp.zeros((1, BW), jnp.float32)

time: 33.8 us -> 33.7 us (level)
  no operation moved by 1% of the time
where the time goes in v5:
time: 33.7 us; the launch traced here: 33.6 us
  Pallas kernels  32.9 us (98%)
  between operations  0.64 us (2%)
    pallas_call x1, Pallas kernels, local(): pl.pallas_call(step_kernel, out_shape=(pltpu.VMEM(tracers.shape, f32), pl...  28.9 us
    pallas_call x1, Pallas kernels, local(): pl.pallas_call(write_kernel, out_shape=(jax.ShapeDtypeStruct(tracers.shap...  4.05 us

profile of v5, /device:TPU:1, one launch (start us, length us, event | category | flops | bytes accessed | tf_op | source)
XLA Modules:
  0.0 33.6 jit_solution(8389748945506269873)
XLA Ops:
  0.6 28.9 %step.1 = (f32[20,4,16,2048]{3,2,1,0:T(8,128)S(1)}, f32[4,16,128]{2,1,0:T(8,128)S(1)}) custom-call(s32[512]{0:T(512)} %cmap_hbm.1, s32[512]{0:T(512)} %tmap_hbm.1, bf16[20,4,2048]{2,1,0:T(4,128)(2,1)} %buoy_hbm.1, s32[4,2048]{1,0:T(4,128)} %wet_hbm.1, s32[4,2048]{1,0:T(4,128)} %patch_hbm.1, f32[4,2048]{1,0:T(4,128)} %prior_hbm.1, s32[4,16,128]{2,1,0:T(8,128)} %land_hbm.1, ...), custom_call_target="tpu_custom_call" | custom-call | tf_op jit(solution)/shard_map/step/pallas_call | solution.py:484
  29.5 4.1 %write.1 = (f32[20,4,16,2048]{3,2,1,0:T(8,128)}, f32[4,16,128]{2,1,0:T(8,128)}) custom-call(f32[20,4,16,2048]{3,2,1,0:T(8,128)S(1)} %get-tuple-element.4.tr, f32[4,16,128]{2,1,0:T(8,128)S(1)} %get-tuple-element.5.height), custom_call_target="tpu_custom_call" | custom-call | tf_op jit(solution)/shard_map/write/pallas_call | solution.py:532

commit v6 on v4

--- a/solution.py
+++ b/solution.py
@@ -20,7 +20,7 @@
 PAIRS = [(i, j) for i in range(ITERS) for j in range(i, ITERS + 1)]
 ENTRIES = 32
 CHUNKS = 8
-PARTS = (range(0, 1), range(1, 5), range(5, 8))
+PARTS = (range(0, 0), range(0, 4), range(4, 8))
 OWN_PART = ((0, 18), (18, 10))
 ROW_PART = ((0, 9), (9, 9))
 DEVICES = NBX * NBY

time: 33.8 us -> 33.8 us (level)
  no operation moved by 1% of the time
where the time goes in v6:
time: 33.8 us; the launch traced here: 33.7 us
  Pallas kernels  33 us (98%)
  between operations  0.64 us (2%)
    pallas_call x1, Pallas kernels, local(): pl.pallas_call(step_kernel, out_shape=(pltpu.VMEM(tracers.shape, f32), pl...  29 us
    pallas_call x1, Pallas kernels, local(): pl.pallas_call(write_kernel, out_shape=(jax.ShapeDtypeStruct(tracers.shap...  4.05 us

profile of v6, /device:TPU:1, one launch (start us, length us, event | category | flops | bytes accessed | tf_op | source)
XLA Modules:
  0.0 33.7 jit_solution(16921058543354803225)
XLA Ops:
  0.6 29.0 %step.1 = (f32[20,4,16,2048]{3,2,1,0:T(8,128)S(1)}, f32[4,16,128]{2,1,0:T(8,128)S(1)}) custom-call(s32[512]{0:T(512)} %cmap_hbm.1, s32[512]{0:T(512)} %tmap_hbm.1, bf16[20,4,2048]{2,1,0:T(4,128)(2,1)} %buoy_hbm.1, s32[4,2048]{1,0:T(4,128)} %wet_hbm.1, s32[4,2048]{1,0:T(4,128)} %patch_hbm.1, f32[4,2048]{1,0:T(4,128)} %prior_hbm.1, s32[4,16,128]{2,1,0:T(8,128)} %land_hbm.1, ...), custom_call_target="tpu_custom_call" | custom-call | tf_op jit(solution)/shard_map/step/pallas_call | solution.py:483
  29.6 4.1 %write.1 = (f32[20,4,16,2048]{3,2,1,0:T(8,128)}, f32[4,16,128]{2,1,0:T(8,128)}) custom-call(f32[20,4,16,2048]{3,2,1,0:T(8,128)S(1)} %get-tuple-element.4.tr, f32[4,16,128]{2,1,0:T(8,128)S(1)} %get-tuple-element.5.height), custom_call_target="tpu_custom_call" | custom-call | tf_op jit(solution)/shard_map/write/pallas_call | solution.py:531
